TPU v7x, 256 devices: a whole 4x4x8 slice. The times are simulated.
256 devices in a mesh: dp: 8 (over y, x_hi), ctx: 32 (over x_lo, z, core).
Axes of the slice: x: 4 (x_hi: 2, x_lo: 2; x = x_hi * 2 + x_lo), y: 4, z: 8, core: 2. Of those that a mesh axis runs over, the one named last changes fastest.
Arguments:
- inputs: bfloat16 [8, 32, 128, 4096], P('dp', 'ctx'), may hold values from -6 to 6
- queries: bfloat16 [8, 32, 128, 1024], P('dp', 'ctx'), may hold values from -6 to 6
- keys_values: bfloat16 [8, 32, 128, 256], P('dp', 'ctx'), may hold values from -6 to 6
- out_grad: bfloat16 [8, 32, 128, 1024], P('dp', 'ctx'), may hold values from -6 to 6
- lengths: int32 [8, 10], P('dp'), may hold values from 1 to 1024, 4096 in all within a row
Outputs:
- grad_q: bfloat16 [8, 32, 128, 1024], P('dp', 'ctx')
- grad_kv: bfloat16 [8, 32, 128, 256], P('dp', 'ctx')
- grad_kv_weight: float32 [4096, 256], P('ctx')
All inputs are finite; a program needn't handle non-finite values.
Results may differ from a plain program's by a relative error of at most 0.0052.
Values may be sent and summed in bfloat16 or wider, within the bound.
A program may use at most 64 MiB of HBM per device.

v0:
```python
import jax
import jax.numpy as jnp
from jax import lax
from jax.sharding import PartitionSpec as P

HD = 128
RESPONSES = 4


neg_fill = -1e30


def from_behind(x, axis, by):
    length = lax.axis_size(axis)
    return lax.ppermute(x, axis, [(i, (i + by) % length) for i in range(length)])


def piece_of(positions, piece_ends):
    return jnp.sum((positions[:, None] >= piece_ends[None, :]).astype(jnp.int32), axis=1)


def allowed_pairs(query_pos, key_pos, piece_ends):
    per_group = RESPONSES + 1
    query_piece = piece_of(query_pos, piece_ends)
    key_piece = piece_of(key_pos, piece_ends)
    same_group = (query_piece // per_group)[:, None] == (key_piece // per_group)[None, :]
    visible = (key_piece % per_group == 0)[None, :] | (query_piece[:, None] == key_piece[None, :])
    return (key_pos[None, :] <= query_pos[:, None]) & same_group & visible


def contract_rows(left_side, right_side):
    return lax.dot_general(
        left_side, right_side, (((0,), (0,)), ((), ())), preferred_element_type=jnp.float32
    )


def on_device(inputs, queries, keys_values, out_grad, lengths):
    stripe_count = lax.axis_size("ctx")
    my_stripe = lax.axis_index("ctx")
    local_count = queries.shape[2]
    q_width = queries.shape[3]
    head_count = q_width // HD
    row_total = local_count * head_count
    score_scale = HD ** (-0.5)
    x_local = inputs[0, 0]
    q_rows = queries[0, 0].reshape(row_total, HD)
    grad_rows = out_grad[0, 0].reshape(row_total, HD)
    kv_local = keys_values[0, 0]
    piece_ends = jnp.cumsum(lengths[0], dtype=jnp.int32)
    query_pos = jnp.arange(local_count, dtype=jnp.int32) * stripe_count + my_stripe

    def row_mask(key_pos):
        key_count = key_pos.shape[0]
        allowed = allowed_pairs(query_pos, key_pos, piece_ends)
        return jnp.broadcast_to(allowed[:, None, :], (local_count, head_count, key_count)).reshape(
            row_total, key_count
        )

    def gathered_pos(first_row, row_count):
        key_rows = first_row + jnp.arange(row_count, dtype=jnp.int32)
        return key_rows % local_count * stripe_count + key_rows // local_count

    def forward_block(carried, kv_block, key_pos):
        running_max, running_sum, weighted = carried
        allowed = row_mask(key_pos)
        scores = (
            jnp.dot(q_rows, kv_block[:, :HD].T, preferred_element_type=jnp.float32) * score_scale
        )
        prob_grad = jnp.dot(grad_rows, kv_block[:, HD:].T, preferred_element_type=jnp.float32)
        new_max = jnp.maximum(running_max, jnp.max(jnp.where(allowed, scores, neg_fill), axis=1))
        factor = jnp.exp(running_max - new_max)
        expo_terms = jnp.where(allowed, jnp.exp(scores - new_max[:, None]), 0.0)
        new_sum = running_sum * factor + jnp.sum(expo_terms, axis=1)
        new_weighted = weighted * factor + jnp.sum(expo_terms * prob_grad, axis=1)
        return (new_max, new_sum, new_weighted)

    init_state = (
        jnp.full((row_total,), neg_fill, jnp.float32),
        jnp.zeros((row_total,), jnp.float32),
        jnp.zeros((row_total,), jnp.float32),
    )
    carried = init_state
    kv_piece = lax.all_gather(kv_local, "ctx", axis=0, tiled=True)
    row_count = kv_piece.shape[0]
    sub_blocks = kv_piece.reshape(row_count // 512, 512, kv_piece.shape[1])

    def inner_step(state_now, sub_item):
        sub_block, sub_index = sub_item
        return (forward_block(state_now, sub_block, gathered_pos(sub_index * 512, 512)), None)

    carried, unused = lax.scan(
        inner_step, carried, (sub_blocks, jnp.arange(row_count // 512, dtype=jnp.int32))
    )
    running_max, running_sum, weighted = carried
    log_total = running_max + jnp.log(running_sum)
    row_delta = weighted / running_sum

    def backward_block(grad_q, kv_block, key_pos):
        allowed = row_mask(key_pos)
        scores = (
            jnp.dot(q_rows, kv_block[:, :HD].T, preferred_element_type=jnp.float32) * score_scale
        )
        soft_probs = jnp.where(allowed, jnp.exp(scores - log_total[:, None]), 0.0)
        prob_grad = jnp.dot(grad_rows, kv_block[:, HD:].T, preferred_element_type=jnp.float32)
        score_grad = soft_probs * (prob_grad - row_delta[:, None])
        low_probs = soft_probs.astype(jnp.bfloat16)
        low_score = score_grad.astype(jnp.bfloat16)
        grad_q = (
            grad_q
            + jnp.dot(low_score, kv_block[:, :HD], preferred_element_type=jnp.float32) * score_scale
        )
        key_term = contract_rows(low_score, q_rows) * score_scale
        value_term = contract_rows(low_probs, grad_rows)
        return (grad_q, jnp.concatenate([key_term, value_term], axis=1))

    zero_grad = jnp.zeros((row_total, HD), jnp.float32)

    def cycle_step(cycle_index, state_now):
        grad_q, kv_block, key_grads = state_now
        source = (my_stripe - cycle_index) % stripe_count
        key_pos = jnp.arange(local_count, dtype=jnp.int32) * stripe_count + source
        grad_q, key_term = backward_block(grad_q, kv_block, key_pos)
        kv_block = from_behind(kv_block, "ctx", 1)
        key_grads = from_behind(key_grads + key_term, "ctx", 1)
        return (grad_q, kv_block, key_grads)

    def cycle_pair(pair_index, state_now):
        return cycle_step(2 * pair_index + 1, cycle_step(2 * pair_index, state_now))

    start_state = (zero_grad, kv_local, jnp.zeros((local_count, 2 * HD), jnp.float32))
    grad_q, spent_kv, key_grads = lax.fori_loop(0, stripe_count // 2, cycle_pair, start_state)
    kv_grad_low = key_grads.astype(jnp.bfloat16)
    grad_q_out = grad_q.astype(jnp.bfloat16).reshape(1, 1, local_count, q_width)
    dp_count = lax.axis_size("dp")
    weight_shard = lax.psum_scatter(
        contract_rows(x_local, kv_grad_low), "ctx", scatter_dimension=0, tiled=True
    )
    weight_total = lax.psum(weight_shard, "dp")
    return (grad_q_out, kv_grad_low.reshape(1, 1, local_count, 2 * HD), weight_total / dp_count)


def solution(mesh):
    return jax.shard_map(
        on_device,
        mesh=mesh,
        in_specs=(
            P("dp", "ctx", None, None),
            P("dp", "ctx", None, None),
            P("dp", "ctx", None, None),
            P("dp", "ctx", None, None),
            P("dp", None),
        ),
        out_specs=(P("dp", "ctx", None, None), P("dp", "ctx", None, None), P("ctx", None)),
        check_vma=False,
    )
```

profile of v0, /device:TPU:32, one launch (start us, length us, event | category | flops | bytes accessed | tf_op | source)
XLA Modules:
  0.0 600.0 jit_solution(14512297040010059716)
XLA Ops:
  12.6 64.4 %all-gather.3.cloned.1.call-done = bf16[1,1,4096,256]{3,2,1,0:T(8,128)(2,1)} async-done(((bf16[1,1,128,256]{3,2,1,0:T(8,128)(2,1)}), bf16[1,1,4096,256]{3,2,1,0:T(8,128)(2,1)}) %all-gather.3.cloned.1.call-update) | async-done | bytes 2097168 | tf_op jit(solution)/shard_map/all_gather | solution.py:83
  77.0 55.5 %while.41 = (s32[]{:T(128)}, f32[1024]{0:T(1024)S(1)}, f32[1024]{0:T(1024)S(1)}, f32[1024]{0:T(1024)S(1)}, s32[8]{0:T(128)S(1)}, /*index=5*/s32[10]{0:T(128)S(1)...) while((s32[]{:T(128)}, f32[1024]{0:T(1024)S(1)}, ...), condition=%wide.region_7.8_spmd.clone, body=%wide.region_1.7_spmd.clone.sunk | while | flops 275166080 | bytes 18316680 | solution.py:91
  132.5 242.1 %while.42 = (s32[]{:T(128)}, f32[1024,128]{1,0:T(8,128)}, bf16[128,256]{1,0:T(8,128)(2,1)S(1)}, f32[128,256]{0,1:T(8,128)S(1)}, s32[]{:T(128)}, /*index=5*/s32[1...) while((s32[]{:T(128)}, f32[1024,128]{1,0:T(8,128)}, ...), condition=%wide.region_12.13_spmd.clone.clone.clone, body=%wide.region_8.12_spmd.clone.clone.clone.sunk | while | flops 338411936 | bytes 14973101 | solution.py:131
  166.1 3.0 collective-permute-done.1
  174.3 3.0 collective-permute-done
  181.7 3.0 collective-permute-done.1
  189.9 3.0 collective-permute-done
  197.3 3.0 collective-permute-done.1
  205.6 3.0 collective-permute-done
  212.9 3.0 collective-permute-done.1
  221.2 3.0 collective-permute-done
  236.8 3.0 collective-permute-done
  252.4 3.0 collective-permute-done
  268.0 3.0 collective-permute-done
  275.4 3.0 collective-permute-done.1
  283.7 3.0 collective-permute-done
  299.3 3.0 collective-permute-done
  314.9 3.0 collective-permute-done
  322.3 3.0 collective-permute-done.1
  330.5 3.0 collective-permute-done
  346.1 3.0 collective-permute-done
  361.8 3.0 collective-permute-done
  377.5 123.0 %reduce-scatter.2.cloned.1.call-done = f32[128,256]{0,1:T(8,128)} async-done(((f32[4096,256]{0,1:T(8,128)}), f32[128,256]{0,1:T(8,128)}) %reduce-scatter.2.cloned.1.call-update) | async-done | bytes 131088 | tf_op jit(solution)/shard_map/reduce_scatter | solution.py:135
  501.4 90.5 %all-reduce.2.cloned.1.call-done = f32[128,256]{0,1:T(8,128)} async-done(((f32[128,256]{0,1:T(8,128)}), f32[128,256]{0,1:T(8,128)}) %all-reduce.2.cloned.1.call-update) | async-done | bytes 131088 | tf_op jit(solution)/shard_map/psum | solution.py:138
  (748 shorter events, 242.3 us)
Async XLA Ops:
  7.2 69.8 %all-gather.3.cloned.1.call-start = ((), (), s32[]{:S(2)}) async-start(), calls=%async_computation.3 | async-start | bytes 2162688 | tf_op jit(solution)/shard_map/all_gather | solution.py:83
  8.8 491.7 %reduce-scatter.2.cloned.1.call-start = ((), (), s32[]{:S(2)}) async-start(), calls=%async_computation.1 | async-start | bytes 4325376 | tf_op jit(solution)/shard_map/reduce_scatter | solution.py:135
  165.0 6.6 %collective-permute-start.3 = (f32[128,256]{0,1:T(8,128)S(1)}, f32[128,256]{0,1:T(8,128)S(1)}, u32[]{:S(2)}, u32[]{:S(2)}) collective-permute-start(f32[128,256]{0,1:T(8,128)S(1)} %maximum_add_fusion.5), channel_id=1, source_target_pairs={{0,1},{1,2},{2,3},{3,4},{4,5},{5,6},{6,7},{7,8},{8,9},{9,10},{10,1... | collective-permute-start | bytes 393224 | tf_op jit(solution)/shard_map/while/body/eval_jaxpr/ppermute | solution.py:15
  174.0 6.6 %collective-permute-start.2 = (f32[128,256]{0,1:T(8,128)S(1)}, f32[128,256]{0,1:T(8,128)S(1)}, u32[]{:S(2)}, u32[]{:S(2)}) collective-permute-start(f32[128,256]{0,1:T(8,128)S(1)} %maximum_add_fusion.4), channel_id=1, source_target_pairs={{0,1},{1,2},{2,3},{3,4},{4,5},{5,6},{6,7},{7,8},{8,9},{9,10},{10,1... | collective-permute-start | bytes 393224 | tf_op jit(solution)/shard_map/while/body/eval_jaxpr/ppermute | solution.py:15
  180.6 6.6 %collective-permute-start.3 = (f32[128,256]{0,1:T(8,128)S(1)}, f32[128,256]{0,1:T(8,128)S(1)}, u32[]{:S(2)}, u32[]{:S(2)}) collective-permute-start(f32[128,256]{0,1:T(8,128)S(1)} %maximum_add_fusion.5), channel_id=1, source_target_pairs={{0,1},{1,2},{2,3},{3,4},{4,5},{5,6},{6,7},{7,8},{8,9},{9,10},{10,1... | collective-permute-start | bytes 393224 | tf_op jit(solution)/shard_map/while/body/eval_jaxpr/ppermute | solution.py:15
  189.6 6.6 %collective-permute-start.2 = (f32[128,256]{0,1:T(8,128)S(1)}, f32[128,256]{0,1:T(8,128)S(1)}, u32[]{:S(2)}, u32[]{:S(2)}) collective-permute-start(f32[128,256]{0,1:T(8,128)S(1)} %maximum_add_fusion.4), channel_id=1, source_target_pairs={{0,1},{1,2},{2,3},{3,4},{4,5},{5,6},{6,7},{7,8},{8,9},{9,10},{10,1... | collective-permute-start | bytes 393224 | tf_op jit(solution)/shard_map/while/body/eval_jaxpr/ppermute | solution.py:15
  196.2 6.6 %collective-permute-start.3 = (f32[128,256]{0,1:T(8,128)S(1)}, f32[128,256]{0,1:T(8,128)S(1)}, u32[]{:S(2)}, u32[]{:S(2)}) collective-permute-start(f32[128,256]{0,1:T(8,128)S(1)} %maximum_add_fusion.5), channel_id=1, source_target_pairs={{0,1},{1,2},{2,3},{3,4},{4,5},{5,6},{6,7},{7,8},{8,9},{9,10},{10,1... | collective-permute-start | bytes 393224 | tf_op jit(solution)/shard_map/while/body/eval_jaxpr/ppermute | solution.py:15
  211.8 6.6 %collective-permute-start.3 = (f32[128,256]{0,1:T(8,128)S(1)}, f32[128,256]{0,1:T(8,128)S(1)}, u32[]{:S(2)}, u32[]{:S(2)}) collective-permute-start(f32[128,256]{0,1:T(8,128)S(1)} %maximum_add_fusion.5), channel_id=1, source_target_pairs={{0,1},{1,2},{2,3},{3,4},{4,5},{5,6},{6,7},{7,8},{8,9},{9,10},{10,1... | collective-permute-start | bytes 393224 | tf_op jit(solution)/shard_map/while/body/eval_jaxpr/ppermute | solution.py:15
  220.9 6.6 %collective-permute-start.2 = (f32[128,256]{0,1:T(8,128)S(1)}, f32[128,256]{0,1:T(8,128)S(1)}, u32[]{:S(2)}, u32[]{:S(2)}) collective-permute-start(f32[128,256]{0,1:T(8,128)S(1)} %maximum_add_fusion.4), channel_id=1, source_target_pairs={{0,1},{1,2},{2,3},{3,4},{4,5},{5,6},{6,7},{7,8},{8,9},{9,10},{10,1... | collective-permute-start | bytes 393224 | tf_op jit(solution)/shard_map/while/body/eval_jaxpr/ppermute | solution.py:15
  227.4 6.6 %collective-permute-start.3 = (f32[128,256]{0,1:T(8,128)S(1)}, f32[128,256]{0,1:T(8,128)S(1)}, u32[]{:S(2)}, u32[]{:S(2)}) collective-permute-start(f32[128,256]{0,1:T(8,128)S(1)} %maximum_add_fusion.5), channel_id=1, source_target_pairs={{0,1},{1,2},{2,3},{3,4},{4,5},{5,6},{6,7},{7,8},{8,9},{9,10},{10,1... | collective-permute-start | bytes 393224 | tf_op jit(solution)/shard_map/while/body/eval_jaxpr/ppermute | solution.py:15
  236.5 6.6 %collective-permute-start.2 = (f32[128,256]{0,1:T(8,128)S(1)}, f32[128,256]{0,1:T(8,128)S(1)}, u32[]{:S(2)}, u32[]{:S(2)}) collective-permute-start(f32[128,256]{0,1:T(8,128)S(1)} %maximum_add_fusion.4), channel_id=1, source_target_pairs={{0,1},{1,2},{2,3},{3,4},{4,5},{5,6},{6,7},{7,8},{8,9},{9,10},{10,1... | collective-permute-start | bytes 393224 | tf_op jit(solution)/shard_map/while/body/eval_jaxpr/ppermute | solution.py:15
  243.1 6.6 %collective-permute-start.3 = (f32[128,256]{0,1:T(8,128)S(1)}, f32[128,256]{0,1:T(8,128)S(1)}, u32[]{:S(2)}, u32[]{:S(2)}) collective-permute-start(f32[128,256]{0,1:T(8,128)S(1)} %maximum_add_fusion.5), channel_id=1, source_target_pairs={{0,1},{1,2},{2,3},{3,4},{4,5},{5,6},{6,7},{7,8},{8,9},{9,10},{10,1... | collective-permute-start | bytes 393224 | tf_op jit(solution)/shard_map/while/body/eval_jaxpr/ppermute | solution.py:15
  252.1 6.6 %collective-permute-start.2 = (f32[128,256]{0,1:T(8,128)S(1)}, f32[128,256]{0,1:T(8,128)S(1)}, u32[]{:S(2)}, u32[]{:S(2)}) collective-permute-start(f32[128,256]{0,1:T(8,128)S(1)} %maximum_add_fusion.4), channel_id=1, source_target_pairs={{0,1},{1,2},{2,3},{3,4},{4,5},{5,6},{6,7},{7,8},{8,9},{9,10},{10,1... | collective-permute-start | bytes 393224 | tf_op jit(solution)/shard_map/while/body/eval_jaxpr/ppermute | solution.py:15
  258.7 6.6 %collective-permute-start.3 = (f32[128,256]{0,1:T(8,128)S(1)}, f32[128,256]{0,1:T(8,128)S(1)}, u32[]{:S(2)}, u32[]{:S(2)}) collective-permute-start(f32[128,256]{0,1:T(8,128)S(1)} %maximum_add_fusion.5), channel_id=1, source_target_pairs={{0,1},{1,2},{2,3},{3,4},{4,5},{5,6},{6,7},{7,8},{8,9},{9,10},{10,1... | collective-permute-start | bytes 393224 | tf_op jit(solution)/shard_map/while/body/eval_jaxpr/ppermute | solution.py:15
  267.7 6.6 %collective-permute-start.2 = (f32[128,256]{0,1:T(8,128)S(1)}, f32[128,256]{0,1:T(8,128)S(1)}, u32[]{:S(2)}, u32[]{:S(2)}) collective-permute-start(f32[128,256]{0,1:T(8,128)S(1)} %maximum_add_fusion.4), channel_id=1, source_target_pairs={{0,1},{1,2},{2,3},{3,4},{4,5},{5,6},{6,7},{7,8},{8,9},{9,10},{10,1... | collective-permute-start | bytes 393224 | tf_op jit(solution)/shard_map/while/body/eval_jaxpr/ppermute | solution.py:15
  274.3 6.6 %collective-permute-start.3 = (f32[128,256]{0,1:T(8,128)S(1)}, f32[128,256]{0,1:T(8,128)S(1)}, u32[]{:S(2)}, u32[]{:S(2)}) collective-permute-start(f32[128,256]{0,1:T(8,128)S(1)} %maximum_add_fusion.5), channel_id=1, source_target_pairs={{0,1},{1,2},{2,3},{3,4},{4,5},{5,6},{6,7},{7,8},{8,9},{9,10},{10,1... | collective-permute-start | bytes 393224 | tf_op jit(solution)/shard_map/while/body/eval_jaxpr/ppermute | solution.py:15
  289.9 6.6 %collective-permute-start.3 = (f32[128,256]{0,1:T(8,128)S(1)}, f32[128,256]{0,1:T(8,128)S(1)}, u32[]{:S(2)}, u32[]{:S(2)}) collective-permute-start(f32[128,256]{0,1:T(8,128)S(1)} %maximum_add_fusion.5), channel_id=1, source_target_pairs={{0,1},{1,2},{2,3},{3,4},{4,5},{5,6},{6,7},{7,8},{8,9},{9,10},{10,1... | collective-permute-start | bytes 393224 | tf_op jit(solution)/shard_map/while/body/eval_jaxpr/ppermute | solution.py:15
  299.0 6.6 %collective-permute-start.2 = (f32[128,256]{0,1:T(8,128)S(1)}, f32[128,256]{0,1:T(8,128)S(1)}, u32[]{:S(2)}, u32[]{:S(2)}) collective-permute-start(f32[128,256]{0,1:T(8,128)S(1)} %maximum_add_fusion.4), channel_id=1, source_target_pairs={{0,1},{1,2},{2,3},{3,4},{4,5},{5,6},{6,7},{7,8},{8,9},{9,10},{10,1... | collective-permute-start | bytes 393224 | tf_op jit(solution)/shard_map/while/body/eval_jaxpr/ppermute | solution.py:15
  305.6 6.6 %collective-permute-start.3 = (f32[128,256]{0,1:T(8,128)S(1)}, f32[128,256]{0,1:T(8,128)S(1)}, u32[]{:S(2)}, u32[]{:S(2)}) collective-permute-start(f32[128,256]{0,1:T(8,128)S(1)} %maximum_add_fusion.5), channel_id=1, source_target_pairs={{0,1},{1,2},{2,3},{3,4},{4,5},{5,6},{6,7},{7,8},{8,9},{9,10},{10,1... | collective-permute-start | bytes 393224 | tf_op jit(solution)/shard_map/while/body/eval_jaxpr/ppermute | solution.py:15
  321.2 6.6 %collective-permute-start.3 = (f32[128,256]{0,1:T(8,128)S(1)}, f32[128,256]{0,1:T(8,128)S(1)}, u32[]{:S(2)}, u32[]{:S(2)}) collective-permute-start(f32[128,256]{0,1:T(8,128)S(1)} %maximum_add_fusion.5), channel_id=1, source_target_pairs={{0,1},{1,2},{2,3},{3,4},{4,5},{5,6},{6,7},{7,8},{8,9},{9,10},{10,1... | collective-permute-start | bytes 393224 | tf_op jit(solution)/shard_map/while/body/eval_jaxpr/ppermute | solution.py:15
  336.8 6.6 %collective-permute-start.3 = (f32[128,256]{0,1:T(8,128)S(1)}, f32[128,256]{0,1:T(8,128)S(1)}, u32[]{:S(2)}, u32[]{:S(2)}) collective-permute-start(f32[128,256]{0,1:T(8,128)S(1)} %maximum_add_fusion.5), channel_id=1, source_target_pairs={{0,1},{1,2},{2,3},{3,4},{4,5},{5,6},{6,7},{7,8},{8,9},{9,10},{10,1... | collective-permute-start | bytes 393224 | tf_op jit(solution)/shard_map/while/body/eval_jaxpr/ppermute | solution.py:15
  352.4 6.6 %collective-permute-start.3 = (f32[128,256]{0,1:T(8,128)S(1)}, f32[128,256]{0,1:T(8,128)S(1)}, u32[]{:S(2)}, u32[]{:S(2)}) collective-permute-start(f32[128,256]{0,1:T(8,128)S(1)} %maximum_add_fusion.5), channel_id=1, source_target_pairs={{0,1},{1,2},{2,3},{3,4},{4,5},{5,6},{6,7},{7,8},{8,9},{9,10},{10,1... | collective-permute-start | bytes 393224 | tf_op jit(solution)/shard_map/while/body/eval_jaxpr/ppermute | solution.py:15
  368.0 6.6 %collective-permute-start.3 = (f32[128,256]{0,1:T(8,128)S(1)}, f32[128,256]{0,1:T(8,128)S(1)}, u32[]{:S(2)}, u32[]{:S(2)}) collective-permute-start(f32[128,256]{0,1:T(8,128)S(1)} %maximum_add_fusion.5), channel_id=1, source_target_pairs={{0,1},{1,2},{2,3},{3,4},{4,5},{5,6},{6,7},{7,8},{8,9},{9,10},{10,1... | collective-permute-start | bytes 393224 | tf_op jit(solution)/shard_map/while/body/eval_jaxpr/ppermute | solution.py:15
  377.4 214.4 %all-reduce.2.cloned.1.call-start = ((), (), s32[]{:S(2)}) async-start(), calls=%async_computation.2 | async-start | bytes 262144 | tf_op jit(solution)/shard_map/psum | solution.py:138
  (119 other events, 955.2 us)
Sparse Core Ops, SparseCore 0:
  10.4 66.4 all-gather.2
  377.6 122.8 reduce-scatter.1
  503.1 88.6 all-reduce.1
where the time goes:
time: 601 us; the launch traced here: 600 us
  waiting for transfers between devices  433 us (72%)
  matrix products  82.5 us (14%)
  local copies, waits for them, and re-layouts  28.8 us (5%)
  other arithmetic  23.3 us (4%)
  between operations  13.9 us (2%)
  starting transfers between devices  10.3 us (2%)
  loops' own time  8.65 us (1%)
    ppermute x64, waiting for transfers between devices, from_behind(): lax.ppermute(x, axis, [(i, (i + by) % length) for i in range(length)])  155 us
    reduce_scatter x1, waiting for transfers between devices, on_device(): lax.psum_scatter(contract_rows(x_local, kv_grad_low), 'ctx', scatter_dime...  123 us
    psum x1, waiting for transfers between devices, on_device(): weight_total = lax.psum(weight_shard, 'dp')  90.5 us
    all_gather x1, waiting for transfers between devices, on_device(): kv_piece = lax.all_gather(kv_local, 'ctx', axis=0, tiled=True)  64.4 us
    dot_general x32, matrix products, backward_block(): jnp.dot(q_rows, kv_block[:, :HD].T, preferred_element_type=jnp.float32)  24.5 us
    dot_general x65, matrix products, contract_rows(): lax.dot_general(left_side, right_side, (((0,), (0,)), ((), ())), preferre...  20.6 us
    dot_general x32, matrix products, backward_block(): jnp.dot(low_score, kv_block[:, :HD], preferred_element_type=jnp.float32)  19.4 us
    reduce_sum x8, other arithmetic, forward_block(): new_sum = running_sum * factor + jnp.sum(expo_terms, axis=1)  13.4 us
  transfers between devices with their start and end apart: 67, of which 65 were waited for; matrix products, arithmetic and copies ran while one was open for 13% of the time, Pallas kernels for 0%

commit v1 on v0

v1 whole, which is shorter than its diff:
```python
import functools
import math

import jax
import jax.numpy as jnp
from jax import lax
from jax.experimental import pallas as pl
from jax.experimental.pallas import tpu as pltpu
from jax.sharding import PartitionSpec as P

HD = 128
HEADS = 8
TOK = 128
STRIPES = 32
NZ = STRIPES // 4
RESPONSES = 4
PIECES = 10
DP = 8
D = 4096
KB = 512
NB = TOK * STRIPES // KB
JB = KB // STRIPES
QI = 32
QR = QI * HEADS
NA = TOK // QI
SCALE = HD ** -0.5
LOG2E = math.log2(math.e)
NEG = -1e30
MESH = pl.DeviceIdType.MESH
BF = jnp.bfloat16
F32 = jnp.float32


def place():
    ctx = lax.axis_index("ctx")
    return ctx // (2 * NZ), (ctx // 2) % NZ, ctx % 2


def index(x, z, c):
    return x * (2 * NZ) + z * 2 + c


def greet(ctx_peers, dp_peers):
    barrier = pltpu.get_barrier_semaphore()
    for peer in ctx_peers:
        pl.semaphore_signal(barrier, inc=1, device_id={"ctx": peer}, device_id_type=MESH)
    for peer in dp_peers:
        pl.semaphore_signal(barrier, inc=1, device_id={"dp": peer}, device_id_type=MESH)
    pl.semaphore_wait(barrier, len(ctx_peers) + len(dp_peers))


def remote(src, dst, send_sem, recv_sem, **device):
    return pltpu.make_async_remote_copy(
        src_ref=src, dst_ref=dst, send_sem=send_sem, recv_sem=recv_sem, device_id=device, device_id_type=MESH
    )


def gather_kernel(kv_ref, x_ref, kvall, xs, own_sem, snd, rcv, xown, xsnd, xrcv):
    x, z, c = place()
    me = index(x, z, c)
    sib, xn, dg = index(x, z, 1 - c), index(1 - x, z, c), index(1 - x, z, 1 - c)
    up, dn = index(x, (z + 1) % NZ, c), index(x, (z + NZ - 1) % NZ, c)
    greet([sib, xn, dg, up, dn], [])
    sends = []

    def send(src, slot, peer):
        copy = remote(src, kvall.at[slot], snd.at[len(sends)], rcv.at[slot], ctx=peer)
        copy.start()
        sends.append(copy)

    def arrive(slot):
        remote(kvall.at[slot], kvall.at[slot], snd.at[0], rcv.at[slot], ctx=sib).wait_recv()

    for peer in (xn, up, dn, sib):
        send(kv_ref, me, peer)
    own = pltpu.make_async_copy(kv_ref, kvall.at[me], own_sem)
    own.start()
    mine = x * 2 + c
    x_copies = []
    for m, (xd, cd) in enumerate(((x, 1 - c), (1 - x, c), (1 - x, 1 - c))):
        for zd in range(NZ):
            cols = pl.ds(pl.multiple_of(index(xd, zd, cd) * HD, HD), HD)
            copy = remote(
                x_ref.at[:, cols],
                xs.at[mine, :, pl.ds(zd * HD, HD)],
                xsnd.at[m, zd],
                xrcv.at[mine, zd],
                ctx=index(xd, z, cd),
            )
            copy.start()
            x_copies.append(copy)
    x_own = []
    for zd in range(NZ):
        cols = pl.ds(pl.multiple_of(index(x, zd, c) * HD, HD), HD)
        copy = pltpu.make_async_copy(x_ref.at[:, cols], xs.at[mine, :, pl.ds(zd * HD, HD)], xown.at[zd])
        copy.start()
        x_own.append(copy)
    other = index(1 - x, z, c)
    arrive(other)
    for peer in (up, dn, sib):
        send(kvall.at[other], other, peer)
    half = NZ // 2
    reach = ((half, half - 1), (half - 1, half))
    for d in range(1, half + 1):
        for side in range(2):
            col = x if side == 0 else 1 - x
            for way in range(2):
                if d > reach[side][way]:
                    continue
                slot = index(col, (z + NZ - d) % NZ if way == 0 else (z + d) % NZ, c)
                arrive(slot)
                if d < reach[side][way]:
                    send(kvall.at[slot], slot, up if way == 0 else dn)
                send(kvall.at[slot], slot, sib)
    for xd in range(2):
        for zd in range(NZ):
            arrive(index(xd, zd, 1 - c))
    own.wait()
    for copy in sends:
        copy.wait_send()
    for copy in x_copies:
        copy.wait_send()
    for copy in x_own:
        copy.wait()
    for m, (xd, cd) in enumerate(((x, 1 - c), (1 - x, c), (1 - x, 1 - c))):
        src = xd * 2 + cd
        for zd in range(NZ):
            ref = xs.at[src, :, pl.ds(zd * HD, HD)]
            remote(ref, ref, xsnd.at[m, zd], xrcv.at[src, zd], ctx=sib).wait_recv()


def gather(kv, x):
    n_sends = 4 + 3 + 4 * (NZ // 2 - 1) * 2 - 2 + 2 * (NZ - 1) + 8
    return pl.pallas_call(
        gather_kernel,
        out_shape=(
            jax.ShapeDtypeStruct((STRIPES, TOK, 2 * HD), BF),
            jax.ShapeDtypeStruct((4, TOK, NZ * HD), BF),
        ),
        in_specs=[pl.BlockSpec(memory_space=pltpu.VMEM), pl.BlockSpec(memory_space=pl.ANY)],
        out_specs=(pl.BlockSpec(memory_space=pltpu.VMEM), pl.BlockSpec(memory_space=pl.ANY)),
        scratch_shapes=[
            pltpu.SemaphoreType.DMA,
            pltpu.SemaphoreType.DMA((n_sends,)),
            pltpu.SemaphoreType.DMA((STRIPES,)),
            pltpu.SemaphoreType.DMA((NZ,)),
            pltpu.SemaphoreType.DMA((3, NZ)),
            pltpu.SemaphoreType.DMA((4, NZ)),
        ],
        compiler_params=pltpu.CompilerParams(collective_id=0, has_side_effects=True, vmem_limit_bytes=40 << 20),
        name="gather_kv",
    )(kv, x)


def dot_t(a, b):
    return lax.dot_general(a, b, (((1,), (1,)), ((), ())), preferred_element_type=F32)


def attention_kernel(len_ref, q_ref, g_ref, kv_ref, gq_ref, dkv_ref, dacc, p_s, pg_s, kt_s, k0_s, mb_s, st_s, gt_s):
    stripe = lax.axis_index("ctx")
    ends = []
    total = jnp.int32(0)
    for k in range(PIECES):
        total = total + len_ref[0, k]
        ends.append(total)
    e0, e4, e5 = ends[0], ends[RESPONSES], ends[RESPONSES + 1]
    row = lax.broadcasted_iota(jnp.int32, (KB, HD), 0)
    k0_s[...] = (row % JB) * STRIPES + row // JB

    def prep(b, carry):
        rows = pl.ds(pl.multiple_of(b * JB, JB), JB)
        kt_s[b] = kv_ref[:, rows, :HD].reshape(KB, HD).T
        dacc[b] = jnp.zeros((KB, 2 * HD), F32)
        return carry

    lax.fori_loop(0, NB, prep, 0)
    c2 = SCALE * LOG2E

    def chunk(a, carry):
        q_rows = pl.ds(pl.multiple_of(a * QI, QI), QI)
        qa = jnp.concatenate([q_ref[q_rows, h * HD : (h + 1) * HD] for h in range(HEADS)], axis=0)
        ga = jnp.concatenate([g_ref[q_rows, h * HD : (h + 1) * HD] for h in range(HEADS)], axis=0)
        lane = lax.broadcasted_iota(jnp.int32, (1, HD), 1)
        pos = (a * QI + lane % QI) * STRIPES + stripe
        first = a * (QI * STRIPES) + stripe
        last = first + (QI - 1) * STRIPES
        start = jnp.zeros((1, HD), jnp.int32)
        start_first = jnp.int32(0)
        for e in ends:
            start = jnp.where(pos >= e, e, start)
            start_first = jnp.where(first >= e, e, start_first)
        prompt_end = jnp.where(pos < e4, e0, e5)
        group_start = jnp.where(pos < e4, 0, e4)

        def needed(b):
            low = b * KB
            high = low + KB - 1
            own = (b >= 2 * a) | (high >= start_first)
            return own | ((first < e4) & (e0 > low)) | ((last >= e4) & (e4 <= high) & (e5 > low))

        st_s[0:1, :] = jnp.full((1, QR), NEG, F32)
        st_s[1:3, :] = jnp.zeros((2, QR), F32)
        gt_s[...] = jnp.zeros((HD, QR), F32)

        def forward(b, carry):
            @pl.when(needed(b))
            def _():
                rows = pl.ds(pl.multiple_of(b * JB, JB), JB)
                key = kv_ref[:, rows, :HD].reshape(KB, HD)
                value = kv_ref[:, rows, HD:].reshape(KB, HD)
                s = dot_t(key, qa)
                pg = dot_t(value, ga)
                pg_s[b] = pg
                k0 = k0_s[...]
                base = b * KB
                mask = (k0 <= pos - base) & (
                    (k0 >= start - base) | ((k0 < prompt_end - base) & (k0 >= group_start - base))
                )
                for half in range(QR // HD):
                    cols = slice(half * HD, (half + 1) * HD)
                    sm = jnp.where(mask, s[:, cols], NEG)
                    m_old = st_s[0:1, cols]
                    m_new = jnp.maximum(m_old, jnp.max(sm, axis=0, keepdims=True))
                    p = jnp.exp2((sm - m_new) * c2)
                    alpha = jnp.exp2((m_old - m_new) * c2)
                    p_s[b, :, cols] = p
                    st_s[0:1, cols] = m_new
                    st_s[1:2, cols] = st_s[1:2, cols] * alpha + jnp.sum(p, axis=0, keepdims=True)
                    st_s[2:3, cols] = st_s[2:3, cols] * alpha + jnp.sum(p * pg[:, cols], axis=0, keepdims=True)
                    mb_s[b, 0:1, cols] = m_new

            return carry

        lax.fori_loop(0, 2 * a + 2, forward, 0)
        m_fin = st_s[0:1, :]
        inv = 1.0 / st_s[1:2, :]
        delta = st_s[2:3, :] * inv

        def backward(b, carry):
            @pl.when(needed(b))
            def _():
                factor = jnp.exp2((mb_s[b, 0:1, :] - m_fin) * c2) * inv
                prob = p_s[b] * factor
                ds = (prob * (pg_s[b] - delta)).astype(BF)
                dacc[b, :, :HD] += jnp.dot(ds, qa, preferred_element_type=F32)
                dacc[b, :, HD:] += jnp.dot(prob.astype(BF), ga, preferred_element_type=F32)
                gt_s[...] += jnp.dot(kt_s[b], ds, preferred_element_type=F32)

            return carry

        lax.fori_loop(0, 2 * a + 2, backward, 0)
        gq = (gt_s[...] * SCALE).T.astype(BF)
        for h in range(HEADS):
            gq_ref[q_rows, h * HD : (h + 1) * HD] = gq[h * QI : (h + 1) * QI]
        return carry

    lax.fori_loop(0, NA, chunk, 0)

    def finish(b, carry):
        rows = pl.ds(pl.multiple_of(b * JB, JB), JB)
        dkv_ref[:, rows, :HD] = (dacc[b, :, :HD] * SCALE).astype(BF).reshape(STRIPES, JB, HD)
        dkv_ref[:, rows, HD:] = dacc[b, :, HD:].astype(BF).reshape(STRIPES, JB, HD)
        return carry

    lax.fori_loop(0, NB, finish, 0)


def attention(lengths, q, g, kvall):
    vmem = pl.BlockSpec(memory_space=pltpu.VMEM)
    return pl.pallas_call(
        attention_kernel,
        out_shape=(
            jax.ShapeDtypeStruct((TOK, HEADS * HD), BF),
            jax.ShapeDtypeStruct((STRIPES, TOK, 2 * HD), BF),
        ),
        in_specs=[pl.BlockSpec(memory_space=pltpu.SMEM), vmem, vmem, vmem],
        out_specs=(vmem, vmem),
        scratch_shapes=[
            pltpu.VMEM((NB, KB, 2 * HD), F32),
            pltpu.VMEM((NB, KB, QR), F32),
            pltpu.VMEM((NB, KB, QR), F32),
            pltpu.VMEM((NB, HD, KB), BF),
            pltpu.VMEM((KB, HD), jnp.int32),
            pltpu.VMEM((NB, 8, QR), F32),
            pltpu.VMEM((8, QR), F32),
            pltpu.VMEM((HD, QR), F32),
        ],
        compiler_params=pltpu.CompilerParams(vmem_limit_bytes=40 << 20),
        name="attention_backward",
    )(lengths, q, g, kvall)


def reduce_kernel(
    dkv, xs_hbm, gkv_ref, w_ref, xs, buf1, sx, buf2, sz, buf3, gs, wt, sw, buf4, w5, buf5,
    xs_sem, s1, r1, s2, r2, s3, r3, s4, r4, s5, r5, s6, r6, s7, r7,
):
    x, z, c = place()
    dp = lax.axis_index("dp")
    mine = x * 2 + c
    sib, xn, dg = index(x, z, 1 - c), index(1 - x, z, c), index(1 - x, z, 1 - c)
    z_peers = [index(x, (z + d) % NZ, c) for d in range(1, NZ)]
    dp_peers = [(dp + d) % DP for d in range(1, DP)]
    load = pltpu.make_async_copy(xs_hbm, xs, xs_sem)
    load.start()
    greet([sib, xn, dg] + z_peers, dp_peers)
    order = sorted(range(NZ), key=lambda d: -min(d, NZ - d))
    targets = [(z + d) % NZ for d in order]
    sends = []
    for col in (1 - x, x):
        for t in targets:
            copy = remote(dkv.at[index(col, t, 1 - c)], buf1.at[col, t], s1.at[col, t], r1.at[col, t], ctx=sib)
            copy.start()
            sends.append(copy)

    def take(ref, recv_sem):
        remote(ref, ref, s1.at[0, 0], recv_sem, ctx=sib).wait_recv()

    for t in targets:
        take(buf1.at[1 - x, t], r1.at[1 - x, t])
        sx[t] = (dkv[index(1 - x, t, c)].astype(F32) + buf1[1 - x, t].astype(F32)).astype(BF)
        copy = remote(sx.at[t], buf2.at[t], s2.at[t], r2.at[t], ctx=xn)
        copy.start()
        sends.append(copy)
    acc = None
    for d, t in zip(order, targets):
        take(buf1.at[x, t], r1.at[x, t])
        take(buf2.at[t], r2.at[t])
        part = dkv[index(x, t, c)].astype(F32) + buf1[x, t].astype(F32) + buf2[t].astype(F32)
        if d == 0:
            acc = part
        else:
            sz[t] = part.astype(BF)
            copy = remote(sz.at[t], buf3.at[z], s3.at[t], r3.at[z], ctx=index(x, t, c))
            copy.start()
            sends.append(copy)
    for t in reversed(targets[:-1]):
        take(buf3.at[t], r3.at[t])
        acc = acc + buf3[t].astype(F32)
    low = acc.astype(BF)
    gs[mine] = low
    for k, peer in enumerate((dg, xn, sib)):
        copy = remote(gs.at[mine], gs.at[mine], s4.at[k], r4.at[mine], ctx=peer)
        copy.start()
        sends.append(copy)
    gkv_ref[...] = low
    load.wait()
    for src in (x * 2 + 1 - c, (1 - x) * 2 + c, (1 - x) * 2 + 1 - c):
        take(gs.at[src], r4.at[src])
    wt[...] = lax.dot_general(
        gs[...].reshape(4 * TOK, 2 * HD),
        xs[...].reshape(4 * TOK, NZ * HD),
        (((0,), (0,)), ((), ())),
        preferred_element_type=F32,
    )
    for d, t in zip(order[:-1], targets[:-1]):
        sw[t] = wt[:, pl.ds(pl.multiple_of(t * HD, HD), HD)].astype(BF)
        copy = remote(sw.at[t], buf4.at[z], s5.at[t], r5.at[z], ctx=index(x, t, c))
        copy.start()
        sends.append(copy)
    total = wt[:, pl.ds(pl.multiple_of(z * HD, HD), HD)]
    for t in reversed(targets[:-1]):
        take(buf4.at[t], r5.at[t])
        total = total + buf4[t].astype(F32)
    rows = HD // DP
    w5[...] = (total.T * (1.0 / DP)).reshape(DP, rows, 2 * HD)
    for peer in dp_peers:
        copy = remote(w5.at[peer], buf5.at[dp], s6.at[peer], r6.at[dp], dp=peer)
        copy.start()
        sends.append(copy)
    part = w5[dp]
    for peer in dp_peers:
        take(buf5.at[peer], r6.at[peer])
        part = part + buf5[peer]
    w_ref[dp] = part
    for peer in dp_peers:
        copy = remote(w_ref.at[dp], w_ref.at[dp], s7.at[peer], r7.at[dp], dp=peer)
        copy.start()
        sends.append(copy)
    for peer in dp_peers:
        take(w_ref.at[peer], r7.at[peer])
    for copy in sends:
        copy.wait_send()


def reduce(dkv, xs):
    vmem = pl.BlockSpec(memory_space=pltpu.VMEM)
    sem = pltpu.SemaphoreType.DMA
    block = (TOK, 2 * HD)
    return pl.pallas_call(
        reduce_kernel,
        out_shape=(
            jax.ShapeDtypeStruct(block, BF),
            jax.ShapeDtypeStruct((DP, HD // DP, 2 * HD), F32),
        ),
        in_specs=[vmem, pl.BlockSpec(memory_space=pl.ANY)],
        out_specs=(vmem, vmem),
        scratch_shapes=[
            pltpu.VMEM((4, TOK, NZ * HD), BF),
            pltpu.VMEM((2, NZ) + block, BF),
            pltpu.VMEM((NZ,) + block, BF),
            pltpu.VMEM((NZ,) + block, BF),
            pltpu.VMEM((NZ,) + block, BF),
            pltpu.VMEM((NZ,) + block, BF),
            pltpu.VMEM((4,) + block, BF),
            pltpu.VMEM((2 * HD, NZ * HD), F32),
            pltpu.VMEM((NZ, 2 * HD, HD), BF),
            pltpu.VMEM((NZ, 2 * HD, HD), BF),
            pltpu.VMEM((DP, HD // DP, 2 * HD), F32),
            pltpu.VMEM((DP, HD // DP, 2 * HD), F32),
            sem,
            sem((2, NZ)), sem((2, NZ)),
            sem((NZ,)), sem((NZ,)),
            sem((NZ,)), sem((NZ,)),
            sem((3,)), sem((4,)),
            sem((NZ,)), sem((NZ,)),
            sem((DP,)), sem((DP,)),
            sem((DP,)), sem((DP,)),
        ],
        compiler_params=pltpu.CompilerParams(collective_id=1, has_side_effects=True, vmem_limit_bytes=40 << 20),
        name="reduce_grads",
    )(dkv, xs)


def on_device(inputs, queries, keys_values, out_grad, lengths):
    kvall, xs = gather(keys_values[0, 0], inputs[0, 0])
    grad_q, dkv = attention(lengths, queries[0, 0], out_grad[0, 0], kvall)
    grad_kv, weight = reduce(dkv, xs)
    return grad_q[None, None], grad_kv[None, None], weight.reshape(HD, 2 * HD)


def solution(mesh):
    return jax.shard_map(
        on_device,
        mesh=mesh,
        in_specs=(
            P("dp", "ctx", None, None),
            P("dp", "ctx", None, None),
            P("dp", "ctx", None, None),
            P("dp", "ctx", None, None),
            P("dp", None),
        ),
        out_specs=(P("dp", "ctx", None, None), P("dp", "ctx", None, None), P("ctx", None)),
        check_vma=False,
    )
```

time: 601 us -> 101 us (0.17)
  waiting for transfers between devices: 433 us -> 0 us
  Pallas kernels: 0 us -> 93.9 us
  matrix products: 82.5 us -> 0 us
  other arithmetic: 23.3 us -> 0 us
  local copies, waits for them, and re-layouts: 28.8 us -> 5.89 us
  between operations: 13.9 us -> 0.67 us
  starting transfers between devices: 10.3 us -> 0 us
  loops' own time: 8.65 us -> 0 us
    ppermute x64 -> x0, waiting for transfers between devices: 155 us -> none  [from_behind(): lax.ppermute(x, axis, [(i, (i + by) % length) for i in range(length)])]
    reduce_scatter x1 -> x0, waiting for transfers between devices: 123 us -> none  [on_device(): lax.psum_scatter(contract_rows(x_local, kv_grad_low), 'ctx', scatter_dime...]
    pallas_call x0 -> x3, Pallas kernels: none -> 93.9 us  [the longest x1 52.2 us: reduce(): pl.pallas_call(reduce_kernel, out_shape=(jax.ShapeDtypeStruct(block, BF),...]
    psum x1 -> x0, waiting for transfers between devices: 90.5 us -> none  [on_device(): weight_total = lax.psum(weight_shard, 'dp')]
    dot_general x177 -> x0, matrix products: 82.5 us -> none  [the longest x32 24.5 us: backward_block(): jnp.dot(q_rows, kv_block[:, :HD].T, preferred_element_type=jnp.float32)]
    all_gather x1 -> x0, waiting for transfers between devices: 64.4 us -> none  [on_device(): kv_piece = lax.all_gather(kv_local, 'ctx', axis=0, tiled=True)]
    reduce_sum x40 -> x0, other arithmetic: 16.2 us -> none  [the longest x8 13.4 us: forward_block(): new_sum = running_sum * factor + jnp.sum(expo_terms, axis=1)]
    ppermute x64 -> x0, starting transfers between devices: 10.2 us -> none  [from_behind(): lax.ppermute(x, axis, [(i, (i + by) % length) for i in range(length)])]
  transfers between devices with their start and end apart: 67 -> 0, of which waited for: 65 -> 0; matrix products, arithmetic and copies ran while one was open for 13% -> 0% of each run, Pallas kernels for 0% -> 0%
where the time goes in v1:
time: 101 us
  Pallas kernels  93.9 us (93%)
  local copies, waits for them, and re-layouts  5.89 us (6%)
    pallas_call x1, Pallas kernels, reduce(): pl.pallas_call(reduce_kernel, out_shape=(jax.ShapeDtypeStruct(block, BF),...  52.2 us
    pallas_call x1, Pallas kernels, gather(): pl.pallas_call(gather_kernel, out_shape=(jax.ShapeDtypeStruct((STRIPES, T...  26.6 us
    pallas_call x1, Pallas kernels, attention(): pl.pallas_call(attention_kernel, out_shape=(jax.ShapeDtypeStruct((TOK, HE...  15.1 us
    unnamed x12, local copies, waits for them, and re-layouts  5.89 us

profile of v1, /device:TPU:32, one launch (start us, length us, event | category | flops | bytes accessed | tf_op | source)
XLA Modules:
  0.0 100.5 jit_solution(3420529457589585953)
XLA Ops:
  0.6 0.0 copy-start
  0.6 1.2 %copy-done = bf16[1,1,128,4096]{3,2,1,0:T(8,128)(2,1)S(1)} copy-done((bf16[1,1,128,4096]{3,2,1,0:T(8,128)(2,1)S(1)}, bf16[1,1,128,4096]{3,2,1,0:T(8,128)(2,1)}, u32[]{:S(2)}) %copy-start) | copy-done | bytes 1048600
  1.9 0.0 copy-start.3
  1.9 0.8 copy-done.3
  2.7 26.6 %gather_kv.1 = (bf16[32,128,256]{2,1,0:T(8,128)(2,1)S(1)}, bf16[4,128,1024]{2,1,0:T(8,128)(2,1)S(1)}) custom-call(bf16[128,256]{1,0:T(8,128)(2,1)S(1)} %bitcast.11, bf16[128,4096]{1,0:T(8,128)(2,1)S(1)} %bitcast.7), custom_call_target="tpu_custom_call" | custom-call | tf_op jit(solution)/shard_map/gather_kv/pallas_call | solution.py:134
  29.3 0.0 copy-start.1
  29.3 0.9 copy-done.1
  30.3 0.0 copy-start.2
  30.3 0.9 copy-done.2
  31.2 0.0 copy-start.4
  31.2 0.7 copy-done.4
  31.9 15.1 %attention_backward.1 = (bf16[128,1024]{1,0:T(8,128)(2,1)}, bf16[32,128,256]{2,1,0:T(8,128)(2,1)S(1)}) custom-call(s32[1,10]{1,0:T(1,128)S(1)} %copy-done.4, bf16[128,1024]{1,0:T(8,128)(2,1)S(1)} %bitcast.8, bf16[128,1024]{1,0:T(8,128)(2,1)S(1)} %bitcast.9, bf16[32,128,256]{2,1,0:T(8,128)(2,1)S(1)} %get-tuple-element.9.kv_ref), custom_call_target="tpu_custom_call" | custom-call | tf_op jit(solution)/shard_map/attention_backward/pallas_call | solution.py:270
  47.0 52.2 %reduce_grads.1 = (bf16[128,256]{1,0:T(8,128)(2,1)S(1)}, f32[8,16,256]{2,1,0:T(8,128)S(1)}) custom-call(bf16[32,128,256]{2,1,0:T(8,128)(2,1)S(1)} %get-tuple-element.11.dkv, bf16[4,128,1024]{2,1,0:T(8,128)(2,1)S(1)} %get-tuple-element.12.xs_hbm), custom_call_target="tpu_custom_call" | custom-call | tf_op jit(solution)/shard_map/reduce_grads/pallas_call | solution.py:389
  99.2 0.6 copy.10
  99.8 0.7 copy.11
Async XLA Ops:
  0.6 1.2 %copy-start = (bf16[1,1,128,4096]{3,2,1,0:T(8,128)(2,1)S(1)}, bf16[1,1,128,4096]{3,2,1,0:T(8,128)(2,1)}, u32[]{:S(2)}) copy-start(bf16[1,1,128,4096]{3,2,1,0:T(8,128)(2,1)} %param.5) | copy-start | bytes 3145732
  1.9 0.8 copy-start.3
  29.3 1.0 copy-start.1
  30.3 0.9 copy-start.2
  31.2 0.7 copy-start.4

commit v2 on v0

v2 whole, which is shorter than its diff:
```python
import functools
import math

import jax
import jax.numpy as jnp
from jax import lax
from jax.experimental import pallas as pl
from jax.experimental.pallas import tpu as pltpu
from jax.sharding import PartitionSpec as P

HD = 128
HEADS = 8
TOK = 128
STRIPES = 32
NZ = STRIPES // 4
RESPONSES = 4
PIECES = 10
DP = 8
D = 4096
QI = 32
QR = QI * HEADS
NA = TOK // QI
HT = TOK // 2
NW = 4
SCALE = HD ** -0.5
LOG2E = math.log2(math.e)
NEG = -1e30
MESH = pl.DeviceIdType.MESH
BF = jnp.bfloat16
F32 = jnp.float32


def place():
    ctx = lax.axis_index("ctx")
    return ctx // (2 * NZ), (ctx // 2) % NZ, ctx % 2


def index(x, z, c):
    return x * (2 * NZ) + z * 2 + c


def greet(ctx_peers, dp_peers):
    barrier = pltpu.get_barrier_semaphore()
    for peer in ctx_peers:
        pl.semaphore_signal(barrier, inc=1, device_id={"ctx": peer}, device_id_type=MESH)
    for peer in dp_peers:
        pl.semaphore_signal(barrier, inc=1, device_id={"dp": peer}, device_id_type=MESH)
    pl.semaphore_wait(barrier, len(ctx_peers) + len(dp_peers))


def remote(src, dst, send_sem, recv_sem, **device):
    return pltpu.make_async_remote_copy(
        src_ref=src, dst_ref=dst, send_sem=send_sem, recv_sem=recv_sem, device_id=device, device_id_type=MESH
    )


def dot_t(a, b):
    return lax.dot_general(a, b, (((1,), (1,)), ((), ())), preferred_element_type=F32)


def t_dot(a, b):
    return lax.dot_general(a, b, (((0,), (0,)), ((), ())), preferred_element_type=F32)


def fused_kernel(
    len_ref, x_ref, q_hbm, kv_hbm, g_hbm, gq_ref, gkv_ref, w_ref,
    q_ref, g_ref, kvall, xs, qa_s, ga_s, k0_s, th_s, st_s, mb_s, p_s, pg_s, dacc, gt_s,
    st1, buf1, sx, buf2, sz, buf3, acc, gs, wt, sw, buf4, wz, sb, buf5, w8,
    in_sem, snd, rcv, xown, xsnd, xrcv, s1, r1, s2, r2, s3, r3, s4, r4, s5, r5, s6, r6, s7, r7,
):
    x, z, c = place()
    dp = lax.axis_index("dp")
    me = index(x, z, c)
    mine = x * 2 + c
    sib, xn, dg = index(x, z, 1 - c), index(1 - x, z, c), index(1 - x, z, 1 - c)
    up, dn = index(x, (z + 1) % NZ, c), index(x, (z + NZ - 1) % NZ, c)
    z_peers = [index(x, (z + d) % NZ, c) for d in range(1, NZ)]
    dp_peers = [(dp + d) % DP for d in range(1, DP)]
    own_kv = pltpu.make_async_copy(kv_hbm, kvall.at[me], in_sem.at[0])
    own_q = pltpu.make_async_copy(q_hbm, q_ref, in_sem.at[1])
    own_g = pltpu.make_async_copy(g_hbm, g_ref, in_sem.at[2])
    for copy in (own_kv, own_q, own_g):
        copy.start()
    greet([sib, xn, dg] + z_peers, dp_peers)
    own_kv.wait()

    def send(slot, peer):
        remote(kvall.at[slot], kvall.at[slot], snd, rcv.at[slot], ctx=peer).start()

    def take(ref, recv_sem):
        remote(ref, ref, snd, recv_sem, ctx=sib).wait_recv()

    def arrive(slot):
        take(kvall.at[slot], rcv.at[slot])

    for peer in (xn, up, dn, sib):
        send(me, peer)
    groups = ((x, 1 - c), (1 - x, c), (1 - x, 1 - c))
    for xd, cd in groups:
        for zd in range(NZ):
            cols = pl.ds(pl.multiple_of(index(xd, zd, cd) * HD, HD), HD)
            dst = xs.at[mine, :, pl.ds(zd * HD, HD)]
            remote(x_ref.at[:, cols], dst, xsnd, xrcv.at[mine], ctx=index(xd, z, cd)).start()
    for zd in range(NZ):
        cols = pl.ds(pl.multiple_of(index(x, zd, c) * HD, HD), HD)
        pltpu.make_async_copy(x_ref.at[:, cols], xs.at[mine, :, pl.ds(zd * HD, HD)], xown).start()

    ends = []
    total_len = jnp.int32(0)
    for k in range(PIECES):
        total_len = total_len + len_ref[0, k]
        ends.append(total_len)
    e0, e4, e5 = ends[0], ends[RESPONSES], ends[RESPONSES + 1]
    shape3 = (4, TOK, HD)
    which = lax.broadcasted_iota(jnp.int32, shape3, 0)
    k0_s[...] = lax.broadcasted_iota(jnp.int32, shape3, 1) * STRIPES + (which // 2) * (2 * NZ) + which % 2
    own_q.wait()
    own_g.wait()
    for a in range(NA):
        q_rows = slice(a * QI, (a + 1) * QI)
        for h in range(HEADS):
            qa_s[a, h * QI : (h + 1) * QI] = q_ref[q_rows, h * HD : (h + 1) * HD]
            ga_s[a, h * QI : (h + 1) * QI] = g_ref[q_rows, h * HD : (h + 1) * HD]
        lane = lax.broadcasted_iota(jnp.int32, (1, HD), 1)
        pos = (a * QI + lane % QI) * STRIPES + me
        start = jnp.zeros((1, HD), jnp.int32)
        for e in ends:
            start = jnp.where(pos >= e, e, start)
        th_s[a, 0:1] = pos
        th_s[a, 1:2] = start
        th_s[a, 2:3] = jnp.where(pos < e4, e0, e5)
        th_s[a, 3:4] = jnp.where(pos < e4, 0, e4)
        st_s[a, 0:1] = jnp.full((1, QR), NEG, F32)
        st_s[a, 1:3] = jnp.zeros((2, QR), F32)
    other = index(1 - x, z, c)
    arrive(other)
    for peer in (up, dn, sib):
        send(other, peer)
    c2 = SCALE * LOG2E
    offsets = [2 * QI * a * (a + 1) for a in range(NA)]

    def keys_of(t, rows, cols):
        pairs = [kvall[pl.ds(2 * t, 2), :rows, cols], kvall[pl.ds(2 * NZ + 2 * t, 2), :rows, cols]]
        return jnp.concatenate(pairs, axis=0).reshape(4 * rows, HD)

    def scores_of(n, carry):
        far = (n + 1) // 2
        t = (z + (1 - n % 2) * far + (n % 2) * (NZ - far)) % NZ
        for xd in range(2):
            arrive(index(xd, t, 1 - c))
        for a in range(NA):
            rows = QI * (a + 1)
            s = dot_t(keys_of(t, rows, slice(0, HD)), qa_s[a])
            pg = dot_t(keys_of(t, rows, slice(HD, 2 * HD)), ga_s[a])
            tile = pl.ds(offsets[a], 4 * rows)
            pg_s[t, tile] = pg
            k0 = k0_s[:, :rows].reshape(4 * rows, HD)
            base = 2 * t
            mask = (k0 <= th_s[a, 0:1] - base) & (
                (k0 >= th_s[a, 1:2] - base) | ((k0 < th_s[a, 2:3] - base) & (k0 >= th_s[a, 3:4] - base))
            )
            for half in range(QR // HD):
                cols = slice(half * HD, (half + 1) * HD)
                sm = jnp.where(mask, s[:, cols], NEG)
                m_old = st_s[a, 0:1, cols]
                m_new = jnp.maximum(m_old, jnp.max(sm, axis=0, keepdims=True))
                p = jnp.exp2((sm - m_new) * c2)
                alpha = jnp.exp2((m_old - m_new) * c2)
                p_s[t, tile, cols] = p
                st_s[a, 0:1, cols] = m_new
                st_s[a, 1:2, cols] = st_s[a, 1:2, cols] * alpha + jnp.sum(p, axis=0, keepdims=True)
                st_s[a, 2:3, cols] = st_s[a, 2:3, cols] * alpha + jnp.sum(p * pg[:, cols], axis=0, keepdims=True)
                mb_s[t, a : a + 1, cols] = m_new
        return carry

    half_z = NZ // 2

    def travel(d, carry):
        below, above = (z + NZ - d) % NZ, (z + d) % NZ
        for way, side in ((0, 0), (1, 0), (0, 1), (1, 1)):
            slot = index(x if side == 0 else 1 - x, below if way == 0 else above, c)
            ahead = up if way == 0 else dn
            reach = half_z if way == side else half_z - 1

            @pl.when(d <= reach)
            def _():
                arrive(slot)

            @pl.when(d < reach)
            def _():
                send(slot, ahead)

            @pl.when(d <= reach)
            def _():
                send(slot, sib)

        lax.fori_loop(jnp.maximum(2 * d - 3, 0), jnp.minimum(2 * d - 1, NZ), scores_of, 0)
        return carry

    lax.fori_loop(1, half_z + 2, travel, 0)

    lane2 = lax.broadcasted_iota(jnp.int32, (1, 2 * HD), 1)
    scale_row = jnp.where(lane2 < HD, SCALE, 1.0).astype(F32)

    def plane_at(k):
        return (z + half_z + (1 - 2 * (k % 2)) * ((k + 1) // 2)) % NZ

    def final_rows(slot, a):
        return dacc[slot, a * QI : (a + 1) * QI] * scale_row

    def to_x(a, t):
        take(buf1.at[a, t], r1.at[a, t])
        sx[a, t] = (final_rows(index(1 - x, t, c), a) + buf1[a, t, 1 - x].astype(F32)).astype(BF)
        remote(sx.at[a, t], buf2.at[a, t], s2, r2.at[a, t], ctx=xn).start()

    def to_z(a, k, t):
        take(buf2.at[a, t], r2.at[a, t])
        val = final_rows(index(x, t, c), a) + buf1[a, t, x].astype(F32) + buf2[a, t].astype(F32)

        @pl.when(k < NZ - 1)
        def _():
            sz[a, k] = val.astype(BF)
            remote(sz.at[a, k], buf3.at[a, z], s3, r3.at[a, z], ctx=index(x, t, c)).start()

        @pl.when(k == NZ - 1)
        def _():
            acc[a] = val

    for a in reversed(range(NA)):
        rows = QI * (a + 1)
        tile = pl.ds(offsets[a], 4 * rows)
        gt_s[...] = jnp.zeros((HD, QR), F32)

        def step(k, carry, a=a, rows=rows, tile=tile):
            t = plane_at(k)
            inv = 1.0 / st_s[a, 1:2]
            delta = st_s[a, 2:3] * inv
            factor = jnp.exp2((mb_s[t, a : a + 1] - st_s[a, 0:1]) * c2) * inv
            prob = p_s[t, tile] * factor
            ds = (prob * (pg_s[t, tile] - delta)).astype(BF)
            dk = jnp.dot(ds, qa_s[a], preferred_element_type=F32).reshape(4, rows, HD)
            dv = jnp.dot(prob.astype(BF), ga_s[a], preferred_element_type=F32).reshape(4, rows, HD)
            for xd in range(2):
                slots = pl.ds(2 * NZ * xd + 2 * t, 2)
                if a == NA - 1:
                    dacc[slots, :rows, :HD] = dk[2 * xd : 2 * xd + 2]
                    dacc[slots, :rows, HD:] = dv[2 * xd : 2 * xd + 2]
                else:
                    dacc[slots, :rows, :HD] += dk[2 * xd : 2 * xd + 2]
                    dacc[slots, :rows, HD:] += dv[2 * xd : 2 * xd + 2]
            gt_s[...] += t_dot(keys_of(t, rows, slice(0, HD)), ds)
            for xd in range(2):
                st1[a, t, xd] = final_rows(index(xd, t, 1 - c), a).astype(BF)
            remote(st1.at[a, t], buf1.at[a, t], s1, r1.at[a, t], ctx=sib).start()
            if a + 1 < NA:
                to_x(a + 1, t)
            if a + 2 < NA:
                to_z(a + 2, k, t)
            return carry

        lax.fori_loop(0, NZ, step, 0)
        gq = (gt_s[...] * SCALE).T.astype(BF)
        for h in range(HEADS):
            gq_ref[a * QI : (a + 1) * QI, h * HD : (h + 1) * HD] = gq[h * QI : (h + 1) * QI]

    def tail(k, carry):
        to_x(0, plane_at(k))
        to_z(1, k, plane_at(k))
        return carry

    lax.fori_loop(0, NZ, tail, 0)

    def settle(a):
        val = acc[a]
        for d in (1, NZ - 1, 2, NZ - 2, 3, NZ - 3, half_z):
            t = (z + d) % NZ
            take(buf3.at[a, t], r3.at[a, t])
            val = val + buf3[a, t].astype(F32)
        piece = slice(a * QI, (a + 1) * QI)
        gs[mine, piece] = val.astype(BF)
        gkv_ref[piece] = val.astype(BF)
        for peer in (dg, xn, sib):
            ref = gs.at[mine, piece]
            remote(ref, ref, s4, r4.at[mine], ctx=peer).start()

    settle(3)
    settle(2)

    def last(k, carry):
        to_z(0, k, plane_at(k))
        return carry

    lax.fori_loop(0, NZ, last, 0)
    settle(1)
    settle(0)
    pltpu.make_async_copy(xs.at[mine], xs.at[mine], xown).wait()
    for xd, cd in groups:
        take(xs.at[xd * 2 + cd], xrcv.at[xd * 2 + cd])
    for xd, cd in groups:
        take(gs.at[xd * 2 + cd], r4.at[xd * 2 + cd])
    sends = []
    group = gs[...].reshape(4 * TOK, 2 * HD)
    rows = 2 * HD // DP
    wide = NZ * HD // NW
    for k in range(NW):
        cols = slice(k * wide, (k + 1) * wide)
        wt[:, cols] = lax.dot_general(
            group,
            xs[:, :, cols].reshape(4 * TOK, wide),
            (((0,), (0,)), ((), ())),
            preferred_element_type=F32,
        )
        sw[:, :, cols] = wt[:, cols].astype(BF).reshape(DP, rows, wide)
        for peer in dp_peers:
            copy = remote(
                sw.at[peer, :, cols], buf4.at[dp, :, cols], s5.at[peer, k], r5.at[dp, k], dp=peer
            )
            copy.start()
            sends.append(copy)
    own_rows = pl.ds(pl.multiple_of(dp * rows, rows), rows)
    for k in range(NW):
        cols = slice(k * wide, (k + 1) * wide)
        part = wt[own_rows, cols]
        for peer in dp_peers:
            take(buf4.at[peer, :, cols], r5.at[peer, k])
            part = part + buf4[peer, :, cols].astype(F32)
        for n in range(wide // HD):
            wz[k * (wide // HD) + n] = part[:, n * HD : (n + 1) * HD]
    targets = [(z + d) % NZ for d in (half_z, 3, NZ - 3, 2, NZ - 2, 1, NZ - 1)]
    for t in targets:
        sb[t] = wz[t].astype(BF)
        copy = remote(sb.at[t], buf5.at[z], s6.at[t], r6.at[z], ctx=index(x, t, c))
        copy.start()
        sends.append(copy)
    total = wz[z]
    for t in reversed(targets):
        take(buf5.at[t], r6.at[t])
        total = total + buf5[t].astype(F32)
    w8[dp] = total * (1.0 / DP)
    for peer in dp_peers:
        copy = remote(w8.at[dp], w8.at[dp], s7.at[peer], r7.at[dp], dp=peer)
        copy.start()
        sends.append(copy)
    for peer in dp_peers:
        take(w8.at[peer], r7.at[peer])
    w_ref[...] = w8[...].reshape(2 * HD, HD).T
    for copy in sends:
        copy.wait_send()

    def sent(ref, sem):
        remote(ref, ref, sem, r1.at[0, 0], ctx=sib).wait_send()

    sent(kvall.at[pl.ds(0, 4 + 3 + 10 + 14)], snd)
    sent(xs.at[pl.ds(0, 3)], xsnd)
    sent(st1, s1)
    sent(sx, s2)
    sent(sz, s3)
    sent(gs.at[pl.ds(0, 3)], s4)


def on_device(inputs, queries, keys_values, out_grad, lengths):
    vmem = pl.BlockSpec(memory_space=pltpu.VMEM)
    hbm = pl.BlockSpec(memory_space=pl.ANY)
    sem = pltpu.SemaphoreType.DMA
    tri = 2 * QI * NA * (NA + 1)
    rows = 2 * HD // DP
    piece = (QI, 2 * HD)
    grad_q, grad_kv, weight = pl.pallas_call(
        fused_kernel,
        out_shape=(
            jax.ShapeDtypeStruct((TOK, HEADS * HD), BF),
            jax.ShapeDtypeStruct((TOK, 2 * HD), BF),
            jax.ShapeDtypeStruct((HD, 2 * HD), F32),
        ),
        in_specs=[pl.BlockSpec(memory_space=pltpu.SMEM), hbm, hbm, hbm, hbm],
        out_specs=(vmem, vmem, vmem),
        scratch_shapes=[
            pltpu.VMEM((TOK, HEADS * HD), BF),
            pltpu.VMEM((TOK, HEADS * HD), BF),
            pltpu.VMEM((STRIPES, TOK, 2 * HD), BF),
            pltpu.VMEM((4, TOK, NZ * HD), BF),
            pltpu.VMEM((NA, QR, HD), BF),
            pltpu.VMEM((NA, QR, HD), BF),
            pltpu.VMEM((4, TOK, HD), jnp.int32),
            pltpu.VMEM((NA, 8, HD), jnp.int32),
            pltpu.VMEM((NA, 8, QR), F32),
            pltpu.VMEM((NZ, 8, QR), F32),
            pltpu.VMEM((NZ, tri, QR), F32),
            pltpu.VMEM((NZ, tri, QR), F32),
            pltpu.VMEM((STRIPES, TOK, 2 * HD), F32),
            pltpu.VMEM((HD, QR), F32),
            pltpu.VMEM((NA, NZ, 2) + piece, BF),
            pltpu.VMEM((NA, NZ, 2) + piece, BF),
            pltpu.VMEM((NA, NZ) + piece, BF),
            pltpu.VMEM((NA, NZ) + piece, BF),
            pltpu.VMEM((NA, NZ - 1) + piece, BF),
            pltpu.VMEM((NA, NZ) + piece, BF),
            pltpu.VMEM((NA,) + piece, F32),
            pltpu.VMEM((4, TOK, 2 * HD), BF),
            pltpu.VMEM((2 * HD, NZ * HD), F32),
            pltpu.VMEM((DP, rows, NZ * HD), BF),
            pltpu.VMEM((DP, rows, NZ * HD), BF),
            pltpu.VMEM((NZ, rows, HD), F32),
            pltpu.VMEM((NZ, rows, HD), BF),
            pltpu.VMEM((NZ, rows, HD), BF),
            pltpu.VMEM((DP, rows, HD), F32),
            sem((3,)),
            sem, sem((STRIPES,)),
            sem, sem, sem((4,)),
            sem, sem((NA, NZ)),
            sem, sem((NA, NZ)),
            sem, sem((NA, NZ)),
            sem, sem((4,)),
            sem((DP, NW)), sem((DP, NW)),
            sem((NZ,)), sem((NZ,)),
            sem((DP,)), sem((DP,)),
        ],
        compiler_params=pltpu.CompilerParams(collective_id=0, has_side_effects=True, vmem_limit_bytes=56 << 20),
        name="fused_backward",
    )(lengths, inputs[0, 0], queries[0, 0], keys_values[0, 0], out_grad[0, 0])
    return grad_q[None, None], grad_kv[None, None], weight


def solution(mesh):
    return jax.shard_map(
        on_device,
        mesh=mesh,
        in_specs=(
            P("dp", "ctx", None, None),
            P("dp", "ctx", None, None),
            P("dp", "ctx", None, None),
            P("dp", "ctx", None, None),
            P("dp", None),
        ),
        out_specs=(P("dp", "ctx", None, None), P("dp", "ctx", None, None), P("ctx", None)),
        check_vma=False,
    )
```

time: 601 us -> 80.8 us (0.13)
  waiting for transfers between devices: 433 us -> 0 us
  matrix products: 82.5 us -> 0 us
  Pallas kernels: 0 us -> 76.2 us
  local copies, waits for them, and re-layouts: 28.8 us -> 3.29 us
  other arithmetic: 23.3 us -> 0 us
  between operations: 13.9 us -> 0.65 us
  starting transfers between devices: 10.3 us -> 0 us
  loops' own time: 8.65 us -> 0 us
    ppermute x64 -> x0, waiting for transfers between devices: 155 us -> none  [from_behind(): lax.ppermute(x, axis, [(i, (i + by) % length) for i in range(length)])]
    reduce_scatter x1 -> x0, waiting for transfers between devices: 123 us -> none  [on_device(): lax.psum_scatter(contract_rows(x_local, kv_grad_low), 'ctx', scatter_dime...]
    psum x1 -> x0, waiting for transfers between devices: 90.5 us -> none  [on_device(): weight_total = lax.psum(weight_shard, 'dp')]
    dot_general x177 -> x0, matrix products: 82.5 us -> none  [the longest x32 24.5 us: backward_block(): jnp.dot(q_rows, kv_block[:, :HD].T, preferred_element_type=jnp.float32)]
    pallas_call x0 -> x1, Pallas kernels: none -> 76.2 us  [on_device(): pl.pallas_call(fused_kernel, out_shape=(jax.ShapeDtypeStruct((TOK, HEADS...]
    all_gather x1 -> x0, waiting for transfers between devices: 64.4 us -> none  [on_device(): kv_piece = lax.all_gather(kv_local, 'ctx', axis=0, tiled=True)]
    reduce_sum x40 -> x0, other arithmetic: 16.2 us -> none  [the longest x8 13.4 us: forward_block(): new_sum = running_sum * factor + jnp.sum(expo_terms, axis=1)]
    ppermute x64 -> x0, starting transfers between devices: 10.2 us -> none  [from_behind(): lax.ppermute(x, axis, [(i, (i + by) % length) for i in range(length)])]
  transfers between devices with their start and end apart: 67 -> 0, of which waited for: 65 -> 0; matrix products, arithmetic and copies ran while one was open for 13% -> 0% of each run, Pallas kernels for 0% -> 0%
where the time goes in v2:
time: 80.8 us; the launch traced here: 80.2 us
  Pallas kernels  76.2 us (94%)
  local copies, waits for them, and re-layouts  3.29 us (4%)
    pallas_call x1, Pallas kernels, on_device(): pl.pallas_call(fused_kernel, out_shape=(jax.ShapeDtypeStruct((TOK, HEADS...  76.2 us
    unnamed x7, local copies, waits for them, and re-layouts  3.29 us

profile of v2, /device:TPU:32, one launch (start us, length us, event | category | flops | bytes accessed | tf_op | source)
XLA Modules:
  0.0 80.2 jit_solution(11672759288242458084)
XLA Ops:
  0.6 76.2 %fused_backward.1 = (bf16[128,1024]{1,0:T(8,128)(2,1)}, bf16[128,256]{1,0:T(8,128)(2,1)}, f32[128,256]{1,0:T(8,128)}) custom-call(s32[1,10]{1,0:T(1,128)} %len_ref.1, bf16[128,4096]{1,0:T(8,128)(2,1)} %bitcast.6, bf16[128,1024]{1,0:T(8,128)(2,1)} %bitcast.8, bf16[128,256]{1,0:T(8,128)(2,1)} %bitcast.10, bf16[128,1024]{1,0:T(8,128)(2,1)} %bitcast.9), custom_call_target="tpu_custom_call" | custom-call | tf_op jit(solution)/shard_map/fused_backward/pallas_call | solution.py:368
  76.9 0.0 copy-start.1
  76.9 1.7 %copy.11 = bf16[1,1,128,1024]{3,2,1,0:T(8,128)(2,1)} copy(bf16[1,1,128,1024]{3,2,1,0:T(8,128)(2,1)} %bitcast.7) | data formatting | bytes 524288
  78.6 0.0 copy-done.1
  78.6 0.0 copy-start
  78.6 0.6 copy.12
  79.2 0.3 copy-done
  79.5 0.7 copy.13
Async XLA Ops:
  76.9 1.7 %copy-start.1 = (bf16[128,256]{1,0:T(8,128)(2,1)S(1)}, bf16[128,256]{1,0:T(8,128)(2,1)}, u32[]{:S(2)}) copy-start(bf16[128,256]{1,0:T(8,128)(2,1)} %get-tuple-element.7) | copy-start | bytes 196612
  78.6 0.9 %copy-start = (f32[128,256]{1,0:T(8,128)S(1)}, f32[128,256]{1,0:T(8,128)}, u32[]{:S(2)}) copy-start(f32[128,256]{1,0:T(8,128)} %get-tuple-element.14) | copy-start | bytes 393220

commit v3 on v2

v3 whole, which is shorter than its diff:
```python
import functools
import math

import jax
import jax.numpy as jnp
from jax import lax
from jax.experimental import pallas as pl
from jax.experimental.pallas import tpu as pltpu
from jax.sharding import PartitionSpec as P

HD = 128
HEADS = 8
TOK = 128
STRIPES = 32
NZ = STRIPES // 4
RESPONSES = 4
PIECES = 10
DP = 8
D = 4096
QI = 32
QH = QI * HEADS
QR = 2 * QH
NA = TOK // QI
HT = TOK // 2
NW = 4
SCALE = HD ** -0.5
LOG2E = math.log2(math.e)
NEG = -1e30
MESH = pl.DeviceIdType.MESH
BF = jnp.bfloat16
F32 = jnp.float32


def place():
    ctx = lax.axis_index("ctx")
    return ctx // (2 * NZ), (ctx // 2) % NZ, ctx % 2


def index(x, z, c):
    return x * (2 * NZ) + z * 2 + c


def greet(ctx_peers, dp_peers):
    barrier = pltpu.get_barrier_semaphore()
    for peer in ctx_peers:
        pl.semaphore_signal(barrier, inc=1, device_id={"ctx": peer}, device_id_type=MESH)
    for peer in dp_peers:
        pl.semaphore_signal(barrier, inc=1, device_id={"dp": peer}, device_id_type=MESH)
    pl.semaphore_wait(barrier, len(ctx_peers) + len(dp_peers))


def remote(src, dst, send_sem, recv_sem, **device):
    return pltpu.make_async_remote_copy(
        src_ref=src, dst_ref=dst, send_sem=send_sem, recv_sem=recv_sem, device_id=device, device_id_type=MESH
    )


def dot_t(a, b):
    return lax.dot_general(a, b, (((1,), (1,)), ((), ())), preferred_element_type=F32)


def t_dot(a, b):
    return lax.dot_general(a, b, (((0,), (0,)), ((), ())), preferred_element_type=F32)


def fused_kernel(
    len_ref, x_ref, q_hbm, kv_hbm, g_hbm, gq_ref, gkv_ref, w_ref,
    q_ref, g_ref, q2_ref, g2_ref, kvall, xs, qa_s, ga_s, k0_s, th_s, st_s, st2, mb_s, p_s, pg_s, dacc, gt_s, gq_mine, gq_buf,
    sx, buf2, sz, buf3, acc, gs, wt, sw, buf4, wz, sb, buf5, w8,
    in_sem, snd, rcv, xown, xsnd, xrcv, qsnd, qrcv, s1, r1, gsnd, grcv, s2, r2, s3, r3, s4, r4, s5, r5, s6, r6, s7, r7,
):
    x, z, c = place()
    dp = lax.axis_index("dp")
    me = index(x, z, c)
    mine = x * 2 + c
    sib, xn, dg = index(x, z, 1 - c), index(1 - x, z, c), index(1 - x, z, 1 - c)
    up, dn = index(x, (z + 1) % NZ, c), index(x, (z + NZ - 1) % NZ, c)
    z_peers = [index(x, (z + d) % NZ, c) for d in range(1, NZ)]
    dp_peers = [(dp + d) % DP for d in range(1, DP)]
    own_kv = pltpu.make_async_copy(kv_hbm, kvall.at[me], in_sem.at[0])
    own_q = pltpu.make_async_copy(q_hbm, q_ref, in_sem.at[1])
    own_g = pltpu.make_async_copy(g_hbm, g_ref, in_sem.at[2])
    for copy in (own_kv, own_q, own_g):
        copy.start()
    greet([sib, xn, dg] + z_peers, dp_peers)
    own_kv.wait()

    def send(slot, h, peer):
        ref = kvall.at[slot, pl.ds(h * HT, HT)]
        remote(ref, ref, snd, rcv.at[slot, h], ctx=peer).start()

    def take(ref, recv_sem):
        remote(ref, ref, snd, recv_sem, ctx=sib).wait_recv()

    def arrive(slot, h):
        take(kvall.at[slot, pl.ds(h * HT, HT)], rcv.at[slot, h])

    for h in range(2):
        for peer in (xn, up, dn):
            send(me, h, peer)
    remote(q_hbm, q2_ref, qsnd.at[0], qrcv.at[0], ctx=sib).start()
    remote(g_hbm, g2_ref, qsnd.at[1], qrcv.at[1], ctx=sib).start()
    groups = ((x, 1 - c), (1 - x, c), (1 - x, 1 - c))
    for xd, cd in groups:
        for zd in range(NZ):
            cols = pl.ds(pl.multiple_of(index(xd, zd, cd) * HD, HD), HD)
            dst = xs.at[mine, :, pl.ds(zd * HD, HD)]
            remote(x_ref.at[:, cols], dst, xsnd, xrcv.at[mine], ctx=index(xd, z, cd)).start()
    for zd in range(NZ):
        cols = pl.ds(pl.multiple_of(index(x, zd, c) * HD, HD), HD)
        pltpu.make_async_copy(x_ref.at[:, cols], xs.at[mine, :, pl.ds(zd * HD, HD)], xown).start()

    ends = []
    total_len = jnp.int32(0)
    for k in range(PIECES):
        total_len = total_len + len_ref[0, k]
        ends.append(total_len)
    e0, e4, e5 = ends[0], ends[RESPONSES], ends[RESPONSES + 1]
    shape3 = (2, TOK, HD)
    which = lax.broadcasted_iota(jnp.int32, shape3, 0)
    k0_s[...] = lax.broadcasted_iota(jnp.int32, shape3, 1) * STRIPES + which * (2 * NZ)
    for a in range(NA):
        lane = lax.broadcasted_iota(jnp.int32, (1, QR), 1)
        pos = (a * QI + lane % QI) * STRIPES + index(x, z, 0) + lane // QH
        start = jnp.zeros((1, QR), jnp.int32)
        for e in ends:
            start = jnp.where(pos >= e, e, start)
        th_s[a, 0:1] = pos
        th_s[a, 1:2] = start
        th_s[a, 2:3] = jnp.where(pos < e4, e0, e5)
        th_s[a, 3:4] = jnp.where(pos < e4, 0, e4)
        st_s[a, 0:1] = jnp.full((1, QR), NEG, F32)
        st_s[a, 1:8] = jnp.zeros((7, QR), F32)
    other = index(1 - x, z, c)
    for h in range(2):
        arrive(other, h)
        for peer in (up, dn):
            send(other, h, peer)
    own_q.wait()
    own_g.wait()
    take(q2_ref, qrcv.at[0])
    take(g2_ref, qrcv.at[1])
    for core, q_in, g_in in ((c, q_ref, g_ref), (1 - c, q2_ref, g2_ref)):
        for a in range(NA):
            q_rows = slice(a * QI, (a + 1) * QI)
            for h in range(HEADS):
                to = pl.ds(pl.multiple_of(core * QH + h * QI, QI), QI)
                qa_s[a, to] = q_in[q_rows, h * HD : (h + 1) * HD]
                ga_s[a, to] = g_in[q_rows, h * HD : (h + 1) * HD]
    c2 = SCALE * LOG2E
    offsets = [QI * a * (a + 1) for a in range(NA)]

    def keys_of(t, rows, cols):
        pair = [kvall[pl.ds(index(xd, t, c), 1), :rows, cols] for xd in range(2)]
        return jnp.concatenate(pair, axis=0).reshape(2 * rows, HD)

    def scores_of(n, carry):
        far = (n + 1) // 2
        t = (z + (1 - n % 2) * far + (n % 2) * (NZ - far)) % NZ
        base = 2 * t + c
        for a in range(NA):
            rows = QI * (a + 1)
            s = dot_t(keys_of(t, rows, slice(0, HD)), qa_s[a])
            pg = dot_t(keys_of(t, rows, slice(HD, 2 * HD)), ga_s[a])
            tile = pl.ds(offsets[a], 2 * rows)
            pg_s[t, tile] = pg
            k0 = k0_s[:, :rows].reshape(2 * rows, HD)
            for core in range(2):
                at = slice(core * QH, core * QH + HD)
                mask = (k0 <= th_s[a, 0:1, at] - base) & (
                    (k0 >= th_s[a, 1:2, at] - base)
                    | ((k0 < th_s[a, 2:3, at] - base) & (k0 >= th_s[a, 3:4, at] - base))
                )
                for half in range(QH // HD):
                    cols = slice(core * QH + half * HD, core * QH + (half + 1) * HD)
                    sm = jnp.where(mask, s[:, cols], NEG)
                    m_old = st_s[a, 0:1, cols]
                    m_new = jnp.maximum(m_old, jnp.max(sm, axis=0, keepdims=True))
                    p = jnp.exp2((sm - m_new) * c2)
                    alpha = jnp.exp2((m_old - m_new) * c2)
                    p_s[t, tile, cols] = p
                    st_s[a, 0:1, cols] = m_new
                    st_s[a, 1:2, cols] = st_s[a, 1:2, cols] * alpha + jnp.sum(p, axis=0, keepdims=True)
                    st_s[a, 2:3, cols] = st_s[a, 2:3, cols] * alpha + jnp.sum(p * pg[:, cols], axis=0, keepdims=True)
                    mb_s[t, a : a + 1, cols] = m_new
        return carry

    half_z = NZ // 2

    def travel(d, carry):
        below, above = (z + NZ - d) % NZ, (z + d) % NZ
        for side in range(2):
            for h in range(2):
                for way in range(2):
                    slot = index(x if side == 0 else 1 - x, below if way == 0 else above, c)
                    reach = half_z if way == side else half_z - 1

                    @pl.when((d > 0) & (d <= reach))
                    def _():
                        arrive(slot, h)

                    @pl.when((d > 0) & (d < reach))
                    def _():
                        send(slot, h, up if way == 0 else dn)

        lax.fori_loop(jnp.maximum(2 * d - 1, 0), jnp.minimum(2 * d + 1, NZ), scores_of, 0)
        return carry

    lax.fori_loop(0, half_z + 1, travel, 0)
    remote(st_s, st2, s1, r1, ctx=sib).start()
    take(st2, r1)
    remote(st_s, st_s, s1, r1, ctx=sib).wait_send()
    for a in range(NA):
        m_fin = jnp.maximum(st_s[a, 0:1], st2[a, 0:1])
        low, high = jnp.exp2((st_s[a, 0:1] - m_fin) * c2), jnp.exp2((st2[a, 0:1] - m_fin) * c2)
        inv = 1.0 / (st_s[a, 1:2] * low + st2[a, 1:2] * high)
        delta = (st_s[a, 2:3] * low + st2[a, 2:3] * high) * inv
        st_s[a, 0:1] = m_fin
        st_s[a, 1:2] = inv
        st_s[a, 2:3] = delta

    lane2 = lax.broadcasted_iota(jnp.int32, (1, 2 * HD), 1)
    scale_row = jnp.where(lane2 < HD, SCALE, 1.0).astype(F32)

    def plane_at(k):
        return (z + half_z + (1 - 2 * (k % 2)) * ((k + 1) // 2)) % NZ

    def final_rows(slot, a):
        return dacc[slot, a * QI : (a + 1) * QI] * scale_row

    def to_x(a, t):
        sx[a, t] = final_rows(index(1 - x, t, c), a).astype(BF)
        remote(sx.at[a, t], buf2.at[a, t], s2, r2.at[a, t], ctx=xn).start()

    def to_z(a, k, t):
        take(buf2.at[a, t], r2.at[a, t])
        val = final_rows(index(x, t, c), a) + buf2[a, t].astype(F32)

        @pl.when(k < NZ - 1)
        def _():
            sz[a, k] = val.astype(BF)
            remote(sz.at[a, k], buf3.at[a, z], s3, r3.at[a, z], ctx=index(x, t, c)).start()

        @pl.when(k == NZ - 1)
        def _():
            acc[a] = val

    own_half = pl.ds(pl.multiple_of(c * QH, QH), QH)
    far_half = pl.ds(pl.multiple_of((1 - c) * QH, QH), QH)
    for a in reversed(range(NA)):
        rows = QI * (a + 1)
        tile = pl.ds(offsets[a], 2 * rows)
        gt_s[a] = jnp.zeros((HD, QR), F32)

        def step(k, carry, a=a, rows=rows, tile=tile):
            t = plane_at(k)
            delta = st_s[a, 2:3]
            factor = jnp.exp2((mb_s[t, a : a + 1] - st_s[a, 0:1]) * c2) * st_s[a, 1:2]
            prob = p_s[t, tile] * factor
            ds = (prob * (pg_s[t, tile] - delta)).astype(BF)
            dk = jnp.dot(ds, qa_s[a], preferred_element_type=F32)
            dv = jnp.dot(prob.astype(BF), ga_s[a], preferred_element_type=F32)
            for xd in range(2):
                slot = index(xd, t, c)
                part = slice(xd * rows, (xd + 1) * rows)
                if a == NA - 1:
                    dacc[slot, :rows, :HD] = dk[part]
                    dacc[slot, :rows, HD:] = dv[part]
                else:
                    dacc[slot, :rows, :HD] += dk[part]
                    dacc[slot, :rows, HD:] += dv[part]
            gt_s[a] += t_dot(keys_of(t, rows, slice(0, HD)), ds)
            to_x(a, t)
            if a + 1 < NA:
                to_z(a + 1, k, t)
            return carry

        lax.fori_loop(0, NZ, step, 0)
        gq_mine[a] = gt_s[a, :, far_half]
        remote(gq_mine.at[a], gq_buf.at[a], gsnd.at[a], grcv.at[a], ctx=sib).start()

    def settle(a):
        val = acc[a]
        for d in (1, NZ - 1, 2, NZ - 2, 3, NZ - 3, half_z):
            t = (z + d) % NZ
            take(buf3.at[a, t], r3.at[a, t])
            val = val + buf3[a, t].astype(F32)
        piece = slice(a * QI, (a + 1) * QI)
        gs[mine, piece] = val.astype(BF)
        gkv_ref[piece] = val.astype(BF)
        for peer in (dg, xn, sib):
            ref = gs.at[mine, piece]
            remote(ref, ref, s4, r4.at[mine], ctx=peer).start()

    def queries_done(a):
        take(gq_buf.at[a], grcv.at[a])
        gq = ((gt_s[a, :, own_half] + gq_buf[a]) * SCALE).T.astype(BF)
        for h in range(HEADS):
            gq_ref[a * QI : (a + 1) * QI, h * HD : (h + 1) * HD] = gq[h * QI : (h + 1) * QI]

    settle(3)
    queries_done(3)

    def last(k, carry):
        to_z(0, k, plane_at(k))
        return carry

    lax.fori_loop(0, NZ, last, 0)
    settle(2)
    settle(1)
    queries_done(2)
    queries_done(1)
    queries_done(0)
    settle(0)
    pltpu.make_async_copy(xs.at[mine], xs.at[mine], xown).wait()
    for xd, cd in groups:
        take(xs.at[xd * 2 + cd], xrcv.at[xd * 2 + cd])
    for xd, cd in groups:
        take(gs.at[xd * 2 + cd], r4.at[xd * 2 + cd])
    sends = []
    group = gs[...].reshape(4 * TOK, 2 * HD)
    rows = 2 * HD // DP
    wide = NZ * HD // NW
    for k in range(NW):
        cols = slice(k * wide, (k + 1) * wide)
        wt[:, cols] = lax.dot_general(
            group,
            xs[:, :, cols].reshape(4 * TOK, wide),
            (((0,), (0,)), ((), ())),
            preferred_element_type=F32,
        )
        sw[:, :, cols] = wt[:, cols].astype(BF).reshape(DP, rows, wide)
        for peer in dp_peers:
            copy = remote(
                sw.at[peer, :, cols], buf4.at[dp, :, cols], s5.at[peer, k], r5.at[dp, k], dp=peer
            )
            copy.start()
            sends.append(copy)
    own_rows = pl.ds(pl.multiple_of(dp * rows, rows), rows)
    per = wide // HD
    for k in range(NW):
        cols = slice(k * wide, (k + 1) * wide)
        part = wt[own_rows, cols]
        for peer in dp_peers:
            take(buf4.at[peer, :, cols], r5.at[peer, k])
            part = part + buf4[peer, :, cols].astype(F32)
        for n in range(per):
            t = k * per + n
            wz[t] = part[:, n * HD : (n + 1) * HD]

            @pl.when(z != t)
            def _():
                sb[t] = wz[t].astype(BF)
                remote(sb.at[t], buf5.at[z], s6.at[t], r6.at[z], ctx=index(x, t, c)).start()

    total = wz[z]
    for d in (1, NZ - 1, 2, NZ - 2, 3, NZ - 3, half_z):
        t = (z + d) % NZ
        take(buf5.at[t], r6.at[t])
        total = total + buf5[t].astype(F32)
        sends.append(remote(sb.at[t], buf5.at[z], s6.at[t], r6.at[z], ctx=index(x, t, c)))
    w8[dp] = total * (1.0 / DP)
    for peer in dp_peers:
        copy = remote(w8.at[dp], w8.at[dp], s7.at[peer], r7.at[dp], dp=peer)
        copy.start()
        sends.append(copy)
    for peer in dp_peers:
        take(w8.at[peer], r7.at[peer])
    w_ref[...] = w8[...].reshape(2 * HD, HD).T
    for copy in sends:
        copy.wait_send()

    def sent(ref, sem):
        remote(ref, ref, sem, r1, ctx=sib).wait_send()

    sent(kvall.at[pl.ds(0, 3 + 2 + 10)], snd)
    sent(q2_ref, qsnd.at[0])
    sent(g2_ref, qsnd.at[1])
    for a in range(NA):
        sent(gq_mine.at[a], gsnd.at[a])
    sent(xs.at[pl.ds(0, 3)], xsnd)
    sent(sx, s2)
    sent(sz, s3)
    sent(gs.at[pl.ds(0, 3)], s4)


def write_kernel(a_in, b_in, c_in, a_out, b_out, c_out):
    a_out[...] = a_in[...]
    b_out[...] = b_in[...]
    c_out[...] = c_in[...]


def write(*arrays):
    vmem = pl.BlockSpec(memory_space=pltpu.VMEM)
    return pl.pallas_call(
        write_kernel,
        out_shape=tuple(jax.ShapeDtypeStruct(a.shape, a.dtype) for a in arrays),
        in_specs=[vmem] * 3,
        out_specs=(vmem,) * 3,
        name="write_results",
    )(*arrays)


def on_device(inputs, queries, keys_values, out_grad, lengths):
    vmem = pl.BlockSpec(memory_space=pltpu.VMEM)
    hbm = pl.BlockSpec(memory_space=pl.ANY)
    sem = pltpu.SemaphoreType.DMA
    tri = QI * NA * (NA + 1)
    rows = 2 * HD // DP
    piece = (QI, 2 * HD)
    grad_q, grad_kv, weight = pl.pallas_call(
        fused_kernel,
        out_shape=(
            jax.ShapeDtypeStruct((TOK, HEADS * HD), BF),
            jax.ShapeDtypeStruct((TOK, 2 * HD), BF),
            jax.ShapeDtypeStruct((HD, 2 * HD), F32),
        ),
        in_specs=[pl.BlockSpec(memory_space=pltpu.SMEM), hbm, hbm, hbm, hbm],
        out_specs=(vmem, vmem, vmem),
        scratch_shapes=[
            pltpu.VMEM((TOK, HEADS * HD), BF),
            pltpu.VMEM((TOK, HEADS * HD), BF),
            pltpu.VMEM((TOK, HEADS * HD), BF),
            pltpu.VMEM((TOK, HEADS * HD), BF),
            pltpu.VMEM((STRIPES, TOK, 2 * HD), BF),
            pltpu.VMEM((4, TOK, NZ * HD), BF),
            pltpu.VMEM((NA, QR, HD), BF),
            pltpu.VMEM((NA, QR, HD), BF),
            pltpu.VMEM((2, TOK, HD), jnp.int32),
            pltpu.VMEM((NA, 8, QR), jnp.int32),
            pltpu.VMEM((NA, 8, QR), F32),
            pltpu.VMEM((NA, 8, QR), F32),
            pltpu.VMEM((NZ, 8, QR), F32),
            pltpu.VMEM((NZ, tri, QR), F32),
            pltpu.VMEM((NZ, tri, QR), F32),
            pltpu.VMEM((STRIPES, TOK, 2 * HD), F32),
            pltpu.VMEM((NA, HD, QR), F32),
            pltpu.VMEM((NA, HD, QH), F32),
            pltpu.VMEM((NA, HD, QH), F32),
            pltpu.VMEM((NA, NZ) + piece, BF),
            pltpu.VMEM((NA, NZ) + piece, BF),
            pltpu.VMEM((NA, NZ - 1) + piece, BF),
            pltpu.VMEM((NA, NZ) + piece, BF),
            pltpu.VMEM((NA,) + piece, F32),
            pltpu.VMEM((4, TOK, 2 * HD), BF),
            pltpu.VMEM((2 * HD, NZ * HD), F32),
            pltpu.VMEM((DP, rows, NZ * HD), BF),
            pltpu.VMEM((DP, rows, NZ * HD), BF),
            pltpu.VMEM((NZ, rows, HD), F32),
            pltpu.VMEM((NZ, rows, HD), BF),
            pltpu.VMEM((NZ, rows, HD), BF),
            pltpu.VMEM((DP, rows, HD), F32),
            sem((3,)),
            sem, sem((STRIPES, 2)),
            sem, sem, sem((4,)),
            sem((2,)), sem((2,)),
            sem, sem,
            sem((NA,)), sem((NA,)),
            sem, sem((NA, NZ)),
            sem, sem((NA, NZ)),
            sem, sem((4,)),
            sem((DP, NW)), sem((DP, NW)),
            sem((NZ,)), sem((NZ,)),
            sem((DP,)), sem((DP,)),
        ],
        compiler_params=pltpu.CompilerParams(collective_id=0, has_side_effects=True, vmem_limit_bytes=56 << 20),
        name="fused_backward",
    )(lengths, inputs[0, 0], queries[0, 0], keys_values[0, 0], out_grad[0, 0])
    grad_q, grad_kv, weight = write(grad_q, grad_kv, weight)
    return grad_q[None, None], grad_kv[None, None], weight


def solution(mesh):
    return jax.shard_map(
        on_device,
        mesh=mesh,
        in_specs=(
            P("dp", "ctx", None, None),
            P("dp", "ctx", None, None),
            P("dp", "ctx", None, None),
            P("dp", "ctx", None, None),
            P("dp", None),
        ),
        out_specs=(P("dp", "ctx", None, None), P("dp", "ctx", None, None), P("ctx", None)),
        check_vma=False,
    )
```

time: 80.8 us -> 71.8 us (0.89)
  Pallas kernels: 76.2 us -> 70.5 us
  local copies, waits for them, and re-layouts: 3.29 us -> 0 us
    pallas_call x1, Pallas kernels: 76.2 us -> 68.7 us  [on_device(): pl.pallas_call(fused_kernel, out_shape=(jax.ShapeDtypeStruct((TOK, HEADS...]
    unnamed x7 -> x0, local copies, waits for them, and re-layouts: 3.29 us -> none
    pallas_call x0 -> x1, Pallas kernels: none -> 1.79 us  [write(): pl.pallas_call(write_kernel, out_shape=tuple((jax.ShapeDtypeStruct(a.shap...]
where the time goes in v3:
time: 71.8 us; the launch traced here: 71.2 us
  Pallas kernels  70.5 us (98%)
    pallas_call x1, Pallas kernels, on_device(): pl.pallas_call(fused_kernel, out_shape=(jax.ShapeDtypeStruct((TOK, HEADS...  68.7 us
    pallas_call x1, Pallas kernels, write(): pl.pallas_call(write_kernel, out_shape=tuple((jax.ShapeDtypeStruct(a.shap...  1.79 us

profile of v3, /device:TPU:32, one launch (start us, length us, event | category | flops | bytes accessed | tf_op | source)
XLA Modules:
  0.0 71.2 jit_solution(12326178993500343437)
XLA Ops:
  0.6 68.7 %fused_backward.1 = (bf16[128,1024]{1,0:T(8,128)(2,1)}, bf16[128,256]{1,0:T(8,128)(2,1)}, f32[128,256]{1,0:T(8,128)}) custom-call(s32[1,10]{1,0:T(1,128)} %len_ref.1, bf16[128,4096]{1,0:T(8,128)(2,1)} %bitcast.6, bf16[128,1024]{1,0:T(8,128)(2,1)} %bitcast.7, bf16[128,256]{1,0:T(8,128)(2,1)} %bitcast.9, bf16[128,1024]{1,0:T(8,128)(2,1)} %bitcast.8), custom_call_target="tpu_custom_call" | custom-call | tf_op jit(solution)/shard_map/fused_backward/pallas_call | solution.py:411
  69.4 1.8 %write_results.1 = (bf16[128,1024]{1,0:T(8,128)(2,1)}, bf16[128,256]{1,0:T(8,128)(2,1)}, f32[128,256]{1,0:T(8,128)}) custom-call(bf16[128,1024]{1,0:T(8,128)(2,1)} %get-tuple-element.9.a_in, bf16[128,256]{1,0:T(8,128)(2,1)} %get-tuple-element.10.b_in, f32[128,256]{1,0:T(8,128)} %get-tuple-element.11.c_in), custom_call_target="tpu_custom_call" | custom-call | tf_op jit(solution)/shard_map/write_results/pallas_call | solution.py:395

commit v4 on v3

--- a/solution.py
+++ b/solution.py
@@ -403,7 +403,7 @@
 
 def on_device(inputs, queries, keys_values, out_grad, lengths):
     vmem = pl.BlockSpec(memory_space=pltpu.VMEM)
-    hbm = pl.BlockSpec(memory_space=pl.ANY)
+    hbm = pl.BlockSpec(memory_space=pltpu.HBM)
     sem = pltpu.SemaphoreType.DMA
     tri = QI * NA * (NA + 1)
     rows = 2 * HD // DP
@@ -463,10 +463,11 @@
             sem((NZ,)), sem((NZ,)),
             sem((DP,)), sem((DP,)),
         ],
-        compiler_params=pltpu.CompilerParams(collective_id=0, has_side_effects=True, vmem_limit_bytes=56 << 20),
+        compiler_params=pltpu.CompilerParams(collective_id=0, has_side_effects=True, vmem_limit_bytes=48 << 20),
         name="fused_backward",
-    )(lengths, inputs[0, 0], queries[0, 0], keys_values[0, 0], out_grad[0, 0])
-    grad_q, grad_kv, weight = write(grad_q, grad_kv, weight)
+    )(pltpu.with_memory_space_constraint(lengths, pltpu.HBM), *(pltpu.with_memory_space_constraint(a[0, 0], pltpu.HBM) for a in (inputs, queries, keys_values, out_grad)))
+    held = [pltpu.with_memory_space_constraint(a, pltpu.VMEM) for a in (grad_q, grad_kv, weight)]
+    grad_q, grad_kv, weight = write(*held)
     return grad_q[None, None], grad_kv[None, None], weight
 
 

time: 71.8 us -> 70 us (0.975)
  Pallas kernels: 70.5 us -> 68.7 us
    pallas_call x1, Pallas kernels: 1.79 us -> 0.79 us  [write(): pl.pallas_call(write_kernel, out_shape=tuple((jax.ShapeDtypeStruct(a.shap...]
    pallas_call x1, Pallas kernels: 68.7 us -> 67.9 us  [on_device(): pl.pallas_call(fused_kernel, out_shape=(jax.ShapeDtypeStruct((TOK, HEADS...]
where the time goes in v4:
time: 70 us; the launch traced here: 69.4 us
  Pallas kernels  68.7 us (98%)
    pallas_call x1, Pallas kernels, on_device(): pl.pallas_call(fused_kernel, out_shape=(jax.ShapeDtypeStruct((TOK, HEADS...  67.9 us

profile of v4, /device:TPU:32, one launch (start us, length us, event | category | flops | bytes accessed | tf_op | source)
XLA Modules:
  0.0 69.4 jit_solution(17196656130227521733)
XLA Ops:
  0.6 67.9 %fused_backward.1 = (bf16[128,1024]{1,0:T(8,128)(2,1)S(1)}, bf16[128,256]{1,0:T(8,128)(2,1)S(1)}, f32[128,256]{1,0:T(8,128)S(1)}) custom-call(s32[1,10]{1,0:T(1,128)} %len_ref.1, bf16[128,4096]{1,0:T(8,128)(2,1)} %bitcast.6, bf16[128,1024]{1,0:T(8,128)(2,1)} %bitcast.7, bf16[128,256]{1,0:T(8,128)(2,1)} %bitcast.9, bf16[128,1024]{1,0:T(8,128)(2,1)} %bitcast.8), custom_call_target="tpu_custom_call" | custom-call | tf_op jit(solution)/shard_map/fused_backward/pallas_call | solution.py:411
  68.6 0.8 %write_results.1 = (bf16[128,1024]{1,0:T(8,128)(2,1)}, bf16[128,256]{1,0:T(8,128)(2,1)}, f32[128,256]{1,0:T(8,128)}) custom-call(bf16[128,1024]{1,0:T(8,128)(2,1)S(1)} %get-tuple-element.9.a_in, bf16[128,256]{1,0:T(8,128)(2,1)S(1)} %get-tuple-element.10.b_in, f32[128,256]{1,0:T(8,128)S(1)} %get-tuple-element.11.c_in), custom_call_target="tpu_custom_call" | custom-call | tf_op jit(solution)/shard_map/write_results/pallas_call | solution.py:395
